TPU v7x, 256 devices: a whole 4x4x8 slice. The times are simulated.
256 devices in a mesh: group: 8 (over z_lo, x), member: 32 (over z_hi, y, core).
Axes of the slice: x: 4, y: 4, z: 8 (z_hi: 4, z_lo: 2; z = z_hi * 2 + z_lo), core: 2. Of those that a mesh axis runs over, the one named last changes fastest.
Arguments:
- entities: bfloat16 [131072, 400], P(('group', 'member')), may hold values from -1.796875 to 1.796875
- hub_rows: bfloat16 [128, 400], replicated, may hold values from -1.796875 to 1.796875
- relations: float32 [2112, 400], replicated
- matching: int32 [8], replicated, may hold values from 0 to 7, as said below
- head_index: int32 [4096, 256], P(('group', 'member')), may hold values from 0 to 511
- tail_index: int32 [4096, 256], P(('group', 'member')), may hold values from 0 to 639
- tile_rel: int32 [4096], P(('group', 'member')), may hold values from 0 to 2111
- tile_count: int32 [8, 32], P('group', 'member'), may hold values from 1 to 16, as said below
Outputs:
- new_entities: bfloat16 [131072, 400], P(('group', 'member'))
- new_hub: bfloat16 [128, 400], replicated
Inputs may be any that keep to these rules, and one draw needn't show every extreme that they name: `matching`: a permutation of the partitions. `tile_count`: some device has exactly 16 live tiles.
All inputs are finite; a program needn't handle non-finite values.
Results may differ from a plain program's by a relative error of at most 0.014.
Values may be sent and summed in bfloat16 or wider, within the bound.
No kernel may reach another device: no remote copies, remote signals or barrier semaphores. Data moves between devices by JAX's collectives and lax.ppermute only.
A program may use at most 64 MiB of HBM per device.

v0:
```python
import jax
import jax.numpy as jnp
from jax import lax
from jax.experimental import pallas as pl
from jax.experimental.pallas import tpu as pltpu
from jax.sharding import PartitionSpec as P

learn_rate = 0.1
BF = jnp.bfloat16
F32 = jnp.float32
LANES = 128
VMEM = pl.BlockSpec(memory_space=pltpu.VMEM)
SMEM = pl.BlockSpec(memory_space=pltpu.SMEM)
HBM = pl.BlockSpec(memory_space=pltpu.HBM)
DMA = pltpu.SemaphoreType.DMA


def hot(ids, rows):
    row = lax.broadcasted_iota(jnp.int32, (rows, ids.shape[1]), 0)
    return jnp.where(row == ids, 1.0, 0.0).astype(BF)


def pair_ids(ids_ref, pair):
    return jnp.concatenate([ids_ref[pl.ds(2 * pair, 1), :], ids_ref[pl.ds(2 * pair + 1, 1), :]], axis=1)


def pick_lane(block, lane):
    lanes = lax.broadcasted_iota(jnp.int32, block.shape, 1)
    return jnp.sum(jnp.where(lanes == lane, block, 0.0), axis=1, keepdims=True)


def dot_nn(a, b):
    return lax.dot_general(a, b, (((1,), (0,)), ((), ())), preferred_element_type=F32)


def dot_nt(a, b):
    return lax.dot_general(a, b, (((1,), (1,)), ((), ())), preferred_element_type=F32)


def dot_tn(a, b):
    return lax.dot_general(a, b, (((0,), (0,)), ((), ())), preferred_element_type=F32)


def weight_kernel(count, rel_ids, rel, weights, table, last, sems):
    live = count[0, 0]
    whole = rel.shape[1] // LANES * LANES
    loads = [pltpu.make_async_copy(rel.at[:, pl.ds(0, whole)], table.at[:, pl.ds(0, whole)], sems.at[0])]
    if whole < rel.shape[1]:
        loads.append(pltpu.make_async_copy(rel.at[:, pl.ds(whole, rel.shape[1] - whole)], last, sems.at[1]))
    for load in loads:
        load.start()
    weights[...] = jnp.zeros_like(weights)
    for load in loads:
        load.wait()
    if whole < rel.shape[1]:
        table[:, whole : rel.shape[1]] = last[...]

    @pl.loop(0, (live + 1) // 2)
    def _(pair):
        total = weights[...]
        lanes = lax.broadcasted_iota(jnp.int32, weights.shape, 1)
        for k in range(2):
            tile = 2 * pair + k
            rid = rel_ids[tile]
            at = rid // LANES * LANES
            w = pick_lane(table[:, pl.ds(pl.multiple_of(at, LANES), LANES)], rid - at)
            total = jnp.where(lanes == tile, jnp.where(tile < live, w, 0.0), total)
        weights[...] = total


def query_kernel(count, ent, heads, weights, query, out, sems):
    live = count[0, 0]
    pairs = 2 * ((live + 3) // 4)
    half, edges = ent.shape[0] // 2, heads.shape[1]

    def put(pair):
        return pltpu.make_async_copy(out.at[pair], query.at[pl.ds(2 * pair, 2)], sems.at[pair])

    @pl.loop(0, pairs)
    def _(pair):
        head = dot_nn(ent[...], hot(pair_ids(heads, pair), ent.shape[1]))
        for k in range(2):
            w = pick_lane(weights[...], 2 * pair + k)
            hr = head[:half, k * edges : (k + 1) * edges]
            hi = head[half:, k * edges : (k + 1) * edges]
            wr, wi = w[:half], w[half:]
            out[pair, k] = jnp.concatenate([hr * wr - hi * wi, hr * wi + hi * wr], axis=0).astype(BF)
        put(pair).start()

    @pl.loop(0, pairs)
    def _(pair):
        put(pair).wait()


def tail_kernel(count, query, partner, hub, tails, pick, diff, grads, table, acc, qin, picks, diffs, moves, qsem, psem, dsem):
    dim, rows = hub.shape[0], partner.shape[1]
    edges = tails.shape[1]
    live = count[0, 0]
    quads = (live + 3) // 4
    pairs = 2 * quads

    def fetch(pair):
        both = pl.ds(2 * pair, 2)
        return pltpu.make_async_copy(query.at[both], qin.at[both], qsem.at[pair])

    def put_pick(pair, slot):
        return pltpu.make_async_copy(picks.at[slot], pick.at[pair], psem.at[slot])

    def put_diff(pair):
        both = pl.ds(2 * pair, 2)
        return pltpu.make_async_copy(diffs.at[both], diff.at[both], dsem.at[pair])

    @pl.loop(0, pairs)
    def _(pair):
        fetch(pair).start()

    table[:, :rows] = partner[:dim]
    table[:, rows:] = hub[...]
    acc[...] = jnp.zeros_like(acc)
    moves[...] = jnp.zeros_like(moves)
    eye = lax.broadcasted_iota(jnp.int32, (edges, edges), 0) == lax.broadcasted_iota(
        jnp.int32, (edges, edges), 1
    )

    def pick_tails(pair, slot):
        picks[slot] = dot_nn(table[...], hot(pair_ids(tails, pair), table.shape[1])).astype(BF)

    def spread(pair, slot):
        acc[...] += dot_nt(moves[slot], hot(pair_ids(tails, pair), table.shape[1]))

    pick_tails(0, 0)
    put_pick(0, 0).start()

    @pl.loop(0, quads)
    def _(quad):
        for slot in range(2):
            pair = 2 * quad + slot
            fetch(pair).wait()

            @pl.when(pair >= 1)
            def _():
                put_pick(pair - 1, 1 - slot).wait()

            ats = [slice(k * edges, (k + 1) * edges) for k in range(2)]
            qs = [qin[2 * pair + k] for k in range(2)]
            scores = [dot_tn(picks[slot, :, ats[k]], qs[k]) for k in range(2)]
            spread(jnp.maximum(pair - 1, 0), 1 - slot)
            ds = []
            for k in range(2):
                tile = 2 * pair + k
                top = jnp.max(scores[k], axis=0, keepdims=True)
                expo = jnp.exp(scores[k] - top)
                probs = expo * (1.0 / jnp.sum(expo, axis=0, keepdims=True))
                d = jnp.where(eye, probs - 1.0, probs)
                if slot + k:
                    d = jnp.where(tile < live, d, 0.0)
                ds.append(d.astype(BF))
                diffs[tile] = ds[k]
            pick_tails(jnp.minimum(pair + 1, pairs - 1), 1 - slot)
            for k in range(2):
                moves[slot, :, ats[k]] = dot_nt(qs[k], ds[k]).astype(BF)
            put_diff(pair).start()

            @pl.when(pair + 1 < pairs)
            def _():
                put_pick(pair + 1, 1 - slot).start()

    spread(pairs - 1, 1)
    chunks, step = grads.shape[0], grads.shape[1]
    for c in range(chunks):
        n = min(step, dim - c * step)
        grads[c, :n] = acc[c * step : c * step + n].astype(BF)
        if n < step:
            grads[c, n:] = jnp.zeros((step - n, grads.shape[2]), BF)
    put_pick(pairs - 1, 1).wait()

    @pl.loop(0, pairs)
    def _(pair):
        put_diff(pair).wait()


def head_kernel(count, pick, diff, weights, heads, ent, base, pin, din, moves, acc, psem, dsem, sem):
    half = acc.shape[0] // 2
    edges = heads.shape[1]
    live = count[0, 0]
    quads = (live + 3) // 4
    pairs = 2 * quads

    def get_pick(pair):
        return pltpu.make_async_copy(pick.at[pair], pin.at[pair], psem.at[pair])

    def get_diff(pair):
        both = pl.ds(2 * pair, 2)
        return pltpu.make_async_copy(diff.at[both], din.at[both], dsem.at[pair])

    @pl.loop(0, pairs)
    def _(pair):
        get_pick(pair).start()
        get_diff(pair).start()

    acc[...] = jnp.zeros_like(acc)
    moves[...] = jnp.zeros_like(moves)

    def spread(pair, slot):
        acc[...] += dot_nt(moves[slot], hot(pair_ids(heads, pair), acc.shape[1]))

    @pl.loop(0, quads)
    def _(quad):
        for slot in range(2):
            pair = 2 * quad + slot
            get_pick(pair).wait()
            get_diff(pair).wait()
            ats = [slice(k * edges, (k + 1) * edges) for k in range(2)]
            d_query = [dot_nn(pin[pair, :, ats[k]], din[2 * pair + k]) for k in range(2)]
            spread(jnp.maximum(pair - 1, 0), 1 - slot)
            for k in range(2):
                w = pick_lane(weights[...], 2 * pair + k)
                dr, di = d_query[k][:half], d_query[k][half:]
                wr, wi = w[:half], w[half:]
                moves[slot, :, ats[k]] = jnp.concatenate(
                    [dr * wr + di * wi, di * wr - dr * wi], axis=0
                ).astype(BF)

    spread(pairs - 1, 1)
    acc[...] = ent[...].astype(F32) - learn_rate * acc[...]
    put = pltpu.make_async_copy(acc, base.at[0], sem)
    put.start()
    put.wait()


def parts_of(dim, step):
    return [(at, min(step, dim - at)) for at in range(0, dim, step)]


def reorder_kernel(matching, rows, out, sems):
    puts = [
        pltpu.make_async_copy(rows.at[matching[g]], out.at[g], sems.at[g]) for g in range(out.shape[0])
    ]
    for put in puts:
        put.start()
    for put in puts:
        put.wait()


def return_kernel(matching, back, hub, base, out, held, sem):
    load = pltpu.make_async_copy(base.at[0], held, sem)
    load.start()
    rows = out.shape[2] - hub.shape[2]
    total = hub[0].astype(F32)
    for m in range(1, hub.shape[0]):
        total += hub[m].astype(F32)
    total = total.astype(BF)
    for g in range(out.shape[0]):
        out[matching[g], :, :rows] = back[g, :, :rows]
        out[g, :, rows:] = total
    load.wait()


def update_kernel(base, hub, last, new_ent, new_hub):
    dim, rows = base.shape
    for i, (at, n) in enumerate(parts_of(dim, last.shape[1])):
        rng = slice(at, at + n)
        got = last[i, :n].astype(F32)
        new_ent[rng] = (base[rng] - learn_rate * got[:, :rows]).astype(BF)
        new_hub[rng] = (hub[rng].astype(F32) - learn_rate * got[:, rows:]).astype(BF)


def call(kernel, out_shape, in_specs, out_specs, flops, moved, scratch=(), exps=0, vmem=32, aliases={}):
    return pl.pallas_call(
        kernel,
        out_shape=out_shape,
        in_specs=in_specs,
        out_specs=out_specs,
        scratch_shapes=scratch,
        input_output_aliases=aliases,
        compiler_params=pltpu.CompilerParams(vmem_limit_bytes=vmem * 1024 * 1024),
        cost_estimate=pl.CostEstimate(flops=flops, bytes_accessed=moved, transcendentals=exps),
    )


shape = jax.ShapeDtypeStruct


def run_weights(tile_count, tile_rel, rel):
    dim, rels = rel.shape
    rest = rels % LANES or LANES
    return call(
        weight_kernel,
        shape((dim, LANES), F32),
        [SMEM, SMEM, HBM],
        VMEM,
        40 * dim * dim * dim,
        4 * rel.size,
        [pltpu.VMEM((dim, -(-rels // LANES) * LANES), F32), pltpu.VMEM((dim, rest), F32), DMA((2,))],
        vmem=60,
    )(tile_count, tile_rel, rel)


def run_query(tile_count, ent, head_index, weights):
    dim, rows = ent.shape
    tiles, edges = head_index.shape
    return call(
        query_kernel,
        shape((2 * tiles, dim, edges), BF),
        [SMEM, VMEM, VMEM, VMEM],
        HBM,
        2 * tiles * edges * dim * rows,
        2 * tiles * dim * edges,
        [pltpu.VMEM((tiles // 2, 2, dim, edges), BF), DMA((tiles // 2,))],
        vmem=60,
    )(tile_count, ent, head_index, weights)


def run_tail(tile_count, query, partner, hub, tail_index, groups, step):
    tiles, edges = tail_index.shape
    dim = query.shape[1]
    rows, hubs = partner.shape[1], hub.shape[1]
    return call(
        tail_kernel,
        [
            shape((tiles, dim, 2 * edges), BF),
            shape((3 * tiles, edges, edges), BF),
            shape((groups, step, rows + hubs), BF),
        ],
        [SMEM, HBM, VMEM, VMEM, VMEM],
        [HBM, HBM, VMEM],
        4 * tiles * edges * dim * (rows + hubs + edges),
        8 * tiles * dim * edges,
        [
            pltpu.VMEM((dim, rows + hubs), BF),
            pltpu.VMEM((dim, rows + hubs), F32),
            pltpu.VMEM((tiles, dim, edges), BF),
            pltpu.VMEM((2, dim, 2 * edges), BF),
            pltpu.VMEM((tiles, edges, edges), BF),
            pltpu.VMEM((2, dim, 2 * edges), BF),
            DMA((tiles // 2,)),
            DMA((2,)),
            DMA((tiles // 2,)),
        ],
        tiles * edges * edges,
        vmem=50,
    )(tile_count, query, partner, hub, tail_index)


def run_head(tile_count, pick, diff, weights, head_index, ent):
    tiles, edges = head_index.shape
    dim, rows = ent.shape
    return call(
        head_kernel,
        shape((8, dim, rows), F32),
        [SMEM, HBM, HBM, VMEM, VMEM, VMEM],
        HBM,
        2 * tiles * edges * dim * (rows + edges),
        6 * tiles * dim * edges,
        [
            pltpu.VMEM((tiles // 2, dim, 2 * edges), BF),
            pltpu.VMEM((tiles, edges, edges), BF),
            pltpu.VMEM((2, dim, 2 * edges), BF),
            pltpu.VMEM((dim, rows), F32),
            DMA((tiles // 2,)),
            DMA((tiles // 2,)),
            DMA(()),
        ],
        vmem=60,
    )(tile_count, pick, diff, weights, head_index, ent)


def make(groups, members):
    def shards(entities, hub_rows, relations, matching, head_index, tail_index, tile_rel, tile_count):
        ent, hub, rel = entities.T, hub_rows.T, relations.T
        dim, rows = ent.shape
        hubs = hub.shape[1]
        step = -(-dim // (8 * groups)) * 8

        high, wide = dim // 8, rows // LANES
        cut = ent.reshape(high, 8, wide, LANES).transpose(0, 2, 1, 3)
        cut = lax.all_to_all(cut.reshape(groups, -1, 8, LANES), "group", 0, 0)
        weights = run_weights(tile_count, tile_rel, rel)
        cut, weights = lax.optimization_barrier((cut, weights))
        cut = call(
            reorder_kernel, shape(cut.shape, BF), [SMEM, VMEM], HBM, 0, 4 * cut.size, [DMA((groups,))]
        )(matching, cut)
        partner = lax.all_to_all(cut, "group", 0, 0).reshape(high, wide, 8, LANES)
        partner = partner.transpose(0, 2, 1, 3).reshape(dim, rows)
        query = run_query(tile_count, ent, head_index, weights)
        pick, diff, grads = run_tail(tile_count, query, partner, hub, tail_index, groups, step)

        got = lax.all_to_all(grads, "group", 0, 0)
        got, pick, diff = lax.optimization_barrier((got, pick, diff))
        part = jnp.sum(got[:, :, rows:].astype(F32), axis=0).astype(BF)
        other = lax.ppermute(part, "member", [(m, m ^ 1) for m in range(members)])
        part = (part.astype(F32) + other.astype(F32)).astype(BF)
        cores = [list(range(core, members, 2)) for core in range(2)]
        parts = jnp.broadcast_to(part[None], (members // 2,) + part.shape)
        parts = lax.all_to_all(parts, "member", 0, 0, axis_index_groups=cores)
        base = run_head(tile_count, pick, diff, weights, head_index, ent)
        parts, base = lax.optimization_barrier((parts, base))
        sent, base = call(
            return_kernel,
            [shape(got.shape, BF), shape((dim, rows), F32)],
            [SMEM, VMEM, VMEM, HBM],
            [VMEM, VMEM],
            0,
            4 * got.size,
            [DMA(())],
            vmem=54,
        )(matching, got, parts, base)
        last = lax.all_to_all(sent, "group", 0, 0)
        new_ent, new_hub = call(
            update_kernel,
            [shape((dim, rows), BF), shape((dim, hubs), BF)],
            [VMEM, VMEM, VMEM],
            [VMEM, VMEM],
            0,
            8 * dim * rows,
        )(base, hub, last)
        return (new_ent.T, new_hub.T)

    return shards


def solution(mesh):
    placed = (
        P(("group", "member"), None),
        P(),
        P(),
        P(),
        P(("group", "member"), None),
        P(("group", "member"), None),
        P(("group", "member")),
        P("group", "member"),
    )
    return jax.shard_map(
        make(mesh.shape["group"], mesh.shape["member"]),
        mesh=mesh,
        in_specs=placed,
        out_specs=(P(("group", "member"), None), P()),
        check_vma=False,
    )
```

profile of v0, /device:TPU:64, one launch (start us, length us, event | category | flops | bytes accessed | tf_op | source)
XLA Modules:
  0.0 94.5 jit_solution(17558647590077171632)
XLA Ops:
  0.6 0.0 copy-start.2
  0.6 5.7 %all-to-all-start = ((bf16[8,25,8,128]{3,2,1,0:T(8,128)(2,1)}), bf16[8,25,8,128]{3,2,1,0:T(8,128)(2,1)S(1)}, u32[]{:S(2)}, u32[]{:S(2)}) async-start(bf16[8,25,8,128]{3,2,1,0:T(8,128)(2,1)} %bitcast.19), calls=%async_computation | async-start | bytes 819200 | tf_op jit(solution)/shard_map/all_to_all | solution.py:377
  7.0 4.1 %shard_map.95.weights = f32[400,128]{1,0:T(8,128)} custom-call(s32[1,1]{1,0:T(1,128)S(6)} %copy.10.count, s32[16]{0:T(128)} %rel_ids.1, f32[400,2112]{1,0:T(8,128)} %bitcast.22), custom_call_target="tpu_custom_call" | custom-call | flops 2560000000 | bytes 3379200 | tf_op jit(solution)/shard_map/pallas_call | solution.py:287
  11.0 0.0 copy-start.1
  11.0 0.0 copy-start.3
  11.0 3.9 %all-to-all-done.rows = bf16[8,25,8,128]{3,2,1,0:T(8,128)(2,1)S(1)} async-done(((bf16[8,25,8,128]{3,2,1,0:T(8,128)(2,1)}), bf16[8,25,8,128]{3,2,1,0:T(8,128)(2,1)S(1)}, u32[]{:S(2)}, u32[]{:S(2)}) %all-to-all-start) | async-done | bytes 409632 | tf_op jit(solution)/shard_map/all_to_all | solution.py:377
  14.9 0.0 copy-done.2
  14.9 1.4 %shard_map.97 = bf16[8,25,8,128]{3,2,1,0:T(8,128)(2,1)} custom-call(s32[8]{0:T(128)S(1)} %copy-done.2, bf16[8,25,8,128]{3,2,1,0:T(8,128)(2,1)S(1)} %all-to-all-done.rows), custom_call_target="tpu_custom_call" | custom-call | bytes 819200 | tf_op jit(solution)/shard_map/pallas_call | solution.py:380
  16.3 3.5 %all-to-all-start.1 = ((bf16[8,25,8,128]{3,2,1,0:T(8,128)(2,1)}), bf16[8,25,8,128]{3,2,1,0:T(8,128)(2,1)S(1)}, u32[]{:S(2)}, u32[]{:S(2)}) async-start(bf16[8,25,8,128]{3,2,1,0:T(8,128)(2,1)} %shard_map.97), calls=%async_computation.1 | async-start | bytes 819200 | tf_op jit(solution)/shard_map/all_to_all | solution.py:383
  19.7 3.6 %shard_map.96.query = bf16[32,400,256]{2,1,0:T(8,128)(2,1)} custom-call(s32[1,1]{1,0:T(1,128)S(6)} %copy.10.count, bf16[400,512]{1,0:T(8,128)(2,1)} %bitcast.20, s32[16,256]{1,0:T(8,128)} %heads.3, f32[400,128]{1,0:T(8,128)} %shard_map.95.weights), custom_call_target="tpu_custom_call" | custom-call | flops 1677721600 | bytes 3276800 | tf_op jit(solution)/shard_map/pallas_call | solution.py:302
  23.4 4.4 %all-to-all-done.1 = bf16[8,25,8,128]{3,2,1,0:T(8,128)(2,1)S(1)} async-done(((bf16[8,25,8,128]{3,2,1,0:T(8,128)(2,1)}), bf16[8,25,8,128]{3,2,1,0:T(8,128)(2,1)S(1)}, u32[]{:S(2)}, u32[]{:S(2)}) %all-to-all-start.1) | async-done | bytes 409632 | tf_op jit(solution)/shard_map/all_to_all | solution.py:383
  27.8 6.4 %shard_map.98 = (bf16[16,400,512]{2,1,0:T(8,128)(2,1)}, bf16[48,256,256]{2,1,0:T(8,128)(2,1)}, bf16[8,56,640]{2,1,0:T(8,128)(2,1)S(1)}) custom-call(s32[1,1]{1,0:T(1,128)S(6)} %copy.10.count, bf16[32,400,256]{2,1,0:T(8,128)(2,1)} %shard_map.96.query, bf16[400,512]{1,0:T(8,128)(2,1)S(1)} %bitcast.16, bf16[400,128]{1,0:T(8,128)(2,1)S(1)} %bitcast.17, ...), custom_call_target="tpu_custom_call" | custom-call | flops 5872025600 | bytes 13107200 | tf_op jit(solution)/shard_map/pallas_call | solution.py:318
  34.2 17.7 %all_to_all.25.back = bf16[8,56,640]{2,1,0:T(8,128)(2,1)S(1)} all-to-all(bf16[8,56,640]{2,1,0:T(8,128)(2,1)S(1)} %get-tuple-element.18), channel_id=1, replica_groups=mesh['group'=8,'member'=32] {'group'}, dimensions={0} | all-to-all | bytes 1146880 | tf_op jit(solution)/shard_map/all_to_all | solution.py:388
  52.0 0.1 collective-permute-start
  52.1 1.2 %collective-permute-done = bf16[56,128]{1,0:T(8,128)(2,1)S(1)} collective-permute-done((bf16[56,128]{1,0:T(8,128)(2,1)S(1)}, bf16[56,128]{1,0:T(8,128)(2,1)S(1)}, u32[]{:S(2)}, u32[]{:S(2)}) %collective-permute-start) | collective-permute-done | bytes 14368 | tf_op jit(solution)/shard_map/ppermute | solution.py:391
  53.2 0.7 broadcast_in_dim.2
  53.9 8.8 %all-to-all-start.3 = ((bf16[16,56,128]{2,1,0:T(8,128)(2,1)}), bf16[16,56,128]{2,1,0:T(8,128)(2,1)S(1)}, u32[]{:S(2)}, u32[]{:S(2)}) async-start(bf16[16,56,128]{2,1,0:T(8,128)(2,1)} %broadcast_in_dim.2), calls=%async_computation.3 | async-start | bytes 458752 | tf_op jit(solution)/shard_map/all_to_all | solution.py:395
  62.7 5.7 %shard_map.99.base = f32[8,400,512]{2,1,0:T(8,128)} custom-call(s32[1,1]{1,0:T(1,128)S(6)} %copy.10.count, bf16[16,400,512]{2,1,0:T(8,128)(2,1)} %get-tuple-element.22.pick, bf16[48,256,256]{2,1,0:T(8,128)(2,1)} %get-tuple-element.23.diff, f32[400,128]{1,0:T(8,128)} %shard_map.95.weights, s32[16,256]{1,0:T(8,128)} %heads.3, bf16[400,512]{1,0:T(8,128)(2,1)} %bitcast.21), custom_call_target="tpu_custom_call" | custom-call | flops 2516582400 | bytes 9830400 | tf_op jit(solution)/shard_map/pallas_call | solution.py:348
  68.5 5.3 %all-to-all-done.3.hub = bf16[16,56,128]{2,1,0:T(8,128)(2,1)S(1)} async-done(((bf16[16,56,128]{2,1,0:T(8,128)(2,1)}), bf16[16,56,128]{2,1,0:T(8,128)(2,1)S(1)}, u32[]{:S(2)}, u32[]{:S(2)}) %all-to-all-start.3) | async-done | bytes 229408 | tf_op jit(solution)/shard_map/all_to_all | solution.py:395
  73.8 0.7 copy-done.5
  74.5 3.4 %shard_map.100 = (bf16[8,56,640]{2,1,0:T(8,128)(2,1)}, f32[400,512]{1,0:T(8,128)}) custom-call(s32[8]{0:T(128)} %matching.3, bf16[8,56,640]{2,1,0:T(8,128)(2,1)} %copy-done.4, bf16[16,56,128]{2,1,0:T(8,128)(2,1)} %copy-done.5, f32[8,400,512]{2,1,0:T(8,128)} %shard_map.99.base), custom_call_target="tpu_custom_call" | custom-call | bytes 1146880 | tf_op jit(solution)/shard_map/pallas_call | solution.py:398
  77.8 14.6 %all_to_all.26.last = bf16[8,56,640]{2,1,0:T(8,128)(2,1)S(1)} all-to-all(bf16[8,56,640]{2,1,0:T(8,128)(2,1)} %get-tuple-element.27), channel_id=1, replica_groups=mesh['group'=8,'member'=32] {'group'}, dimensions={0} | all-to-all | bytes 1146880 | tf_op jit(solution)/shard_map/all_to_all | solution.py:408
  92.4 1.1 %copy-done = f32[400,512]{1,0:T(8,128)S(1)} copy-done((f32[400,512]{1,0:T(8,128)S(1)}, f32[400,512]{1,0:T(8,128)}, u32[]{:S(2)}) %copy-start) | copy-done | bytes 819224
  93.6 0.9 shard_map.101
  (8 shorter events, 0.0 us)
Async XLA Ops:
  0.6 14.3 %copy-start.2 = (s32[8]{0:T(128)S(1)}, s32[8]{0:T(128)}, u32[]{:S(2)}) copy-start(s32[8]{0:T(128)} %matching.3) | copy-start | bytes 100
  0.6 14.3 %all-to-all-start = ((bf16[8,25,8,128]{3,2,1,0:T(8,128)(2,1)}), bf16[8,25,8,128]{3,2,1,0:T(8,128)(2,1)S(1)}, u32[]{:S(2)}, u32[]{:S(2)}) async-start(bf16[8,25,8,128]{3,2,1,0:T(8,128)(2,1)} %bitcast.19), calls=%async_computation | async-start | bytes 819200 | tf_op jit(solution)/shard_map/all_to_all | solution.py:377
  11.0 16.8 %copy-start.1 = (bf16[128,400]{0,1:T(8,128)(2,1)S(1)}, bf16[128,400]{0,1:T(8,128)(2,1)}, u32[]{:S(2)}) copy-start(bf16[128,400]{0,1:T(8,128)(2,1)} %param.9) | copy-start | bytes 307204
  11.0 16.8 %copy-start.3 = (s32[16,256]{1,0:T(8,128)S(1)}, s32[16,256]{1,0:T(8,128)}, u32[]{:S(2)}) copy-start(s32[16,256]{1,0:T(8,128)} %tails.1) | copy-start | bytes 49156
  16.3 11.6 %all-to-all-start.1 = ((bf16[8,25,8,128]{3,2,1,0:T(8,128)(2,1)}), bf16[8,25,8,128]{3,2,1,0:T(8,128)(2,1)S(1)}, u32[]{:S(2)}, u32[]{:S(2)}) async-start(bf16[8,25,8,128]{3,2,1,0:T(8,128)(2,1)} %shard_map.97), calls=%async_computation.1 | async-start | bytes 819200 | tf_op jit(solution)/shard_map/all_to_all | solution.py:383
  51.9 16.6 %copy-start.4 = (bf16[8,56,640]{2,1,0:T(8,128)(2,1)}, bf16[8,56,640]{2,1,0:T(8,128)(2,1)S(1)}, u32[]{:S(2)}) copy-start(bf16[8,56,640]{2,1,0:T(8,128)(2,1)S(1)} %all_to_all.25.back) | copy-start | bytes 1720324
  52.0 1.3 %collective-permute-start = (bf16[56,128]{1,0:T(8,128)(2,1)S(1)}, bf16[56,128]{1,0:T(8,128)(2,1)S(1)}, u32[]{:S(2)}, u32[]{:S(2)}) collective-permute-start(bf16[56,128]{1,0:T(8,128)(2,1)S(1)} %slice_reduce_fusion), channel_id=1, source_target_pairs={{0,1},{1,0},{2,3},{3,2},{4,5},{5,4},{6,7},{7,6},{8,9},{9,8},{10,11... | collective-permute-start | bytes 43016 | tf_op jit(solution)/shard_map/ppermute | solution.py:391
  53.9 19.8 %all-to-all-start.3 = ((bf16[16,56,128]{2,1,0:T(8,128)(2,1)}), bf16[16,56,128]{2,1,0:T(8,128)(2,1)S(1)}, u32[]{:S(2)}, u32[]{:S(2)}) async-start(bf16[16,56,128]{2,1,0:T(8,128)(2,1)} %broadcast_in_dim.2), calls=%async_computation.3 | async-start | bytes 458752 | tf_op jit(solution)/shard_map/all_to_all | solution.py:395
  73.8 0.7 copy-start.5
  92.4 1.1 %copy-start = (f32[400,512]{1,0:T(8,128)S(1)}, f32[400,512]{1,0:T(8,128)}, u32[]{:S(2)}) copy-start(f32[400,512]{1,0:T(8,128)} %get-tuple-element.26.base) | copy-start | bytes 2457604
where the time goes:
time: 95.5 us; the launch traced here: 94.5 us
  blocking collectives  32.3 us (34%)
  Pallas kernels  25.4 us (27%)
  starting transfers between devices  18 us (19%)
  waiting for transfers between devices  14.7 us (15%)
  local copies, waits for them, and re-layouts  2.57 us (3%)
  between operations  1.39 us (1%)
    all_to_all x1, blocking collectives, shards(): got = lax.all_to_all(grads, 'group', 0, 0)  17.7 us
    all_to_all x1, blocking collectives, shards(): last = lax.all_to_all(sent, 'group', 0, 0)  14.6 us
    all_to_all x1, starting transfers between devices, shards(): parts = lax.all_to_all(parts, 'member', 0, 0, axis_index_groups=cores)  8.79 us
    pallas_call x1, Pallas kernels, run_tail(): call(tail_kernel, [shape((tiles, dim, 2 * edges), BF), shape((3 * tiles,...  6.36 us
    pallas_call x1, Pallas kernels, run_head(): call(head_kernel, shape((8, dim, rows), F32), [SMEM, HBM, HBM, VMEM, VMEM...  5.75 us
    all_to_all x1, starting transfers between devices, shards(): cut = lax.all_to_all(cut.reshape(groups, -1, 8, LANES), 'group', 0, 0)  5.67 us
    all_to_all x1, waiting for transfers between devices, shards(): parts = lax.all_to_all(parts, 'member', 0, 0, axis_index_groups=cores)  5.28 us
    all_to_all x1, waiting for transfers between devices, shards(): partner = lax.all_to_all(cut, 'group', 0, 0).reshape(high, wide, 8, LANES)  4.43 us
  transfers between devices with their start and end apart: 4, of which 4 were waited for; matrix products, arithmetic and copies ran while one was open for 0% of the time, Pallas kernels for 14%

commit v1 on v0

--- a/solution.py
+++ b/solution.py
@@ -403,7 +403,7 @@
             0,
             4 * got.size,
             [DMA(())],
-            vmem=54,
+            vmem=50,
         )(matching, got, parts, base)
         last = lax.all_to_all(sent, "group", 0, 0)
         new_ent, new_hub = call(

time: 95.5 us -> 91.2 us (0.955)
  Pallas kernels: 25.4 us -> 18.9 us
  starting transfers between devices: 18 us -> 20.7 us
  waiting for transfers between devices: 14.7 us -> 17.2 us
  local copies, waits for them, and re-layouts: 2.57 us -> 0.74 us
    all_to_all x1, starting transfers between devices: 8.79 us -> 11.4 us  [shards(): parts = lax.all_to_all(parts, 'member', 0, 0, axis_index_groups=cores)]
    pallas_call x1, Pallas kernels: 6.36 us -> 4.04 us  [run_tail(): call(tail_kernel, [shape((tiles, dim, 2 * edges), BF), shape((3 * tiles,...]
    unnamed x12 -> x6, local copies, waits for them, and re-layouts: 1.85 us -> 0.02 us
    pallas_call x1, Pallas kernels: 3.36 us -> 1.69 us  [shards(): call(return_kernel, [shape(got.shape, BF), shape((dim, rows), F32)], [SME...]
    all_to_all x1, blocking collectives: 14.6 us -> 13.5 us  [shards(): last = lax.all_to_all(sent, 'group', 0, 0)]
    all_to_all x1, waiting for transfers between devices: 5.28 us -> 6.34 us  [shards(): parts = lax.all_to_all(parts, 'member', 0, 0, axis_index_groups=cores)]
    pallas_call x1, Pallas kernels: 5.75 us -> 4.69 us  [run_head(): call(head_kernel, shape((8, dim, rows), F32), [SMEM, HBM, HBM, VMEM, VMEM...]
  transfers between devices with their start and end apart: 4 -> 4, of which waited for: 4 -> 4; matrix products, arithmetic and copies ran while one was open for 0% -> 0% of each run, Pallas kernels for 14% -> 12%
where the time goes in v1:
time: 91.2 us; the launch traced here: 90.8 us
  blocking collectives  31.8 us (35%)
  starting transfers between devices  20.7 us (23%)
  Pallas kernels  18.9 us (21%)
  waiting for transfers between devices  17.2 us (19%)
  between operations  1.38 us (2%)
    all_to_all x1, blocking collectives, shards(): got = lax.all_to_all(grads, 'group', 0, 0)  18.3 us
    all_to_all x1, blocking collectives, shards(): last = lax.all_to_all(sent, 'group', 0, 0)  13.5 us
    all_to_all x1, starting transfers between devices, shards(): parts = lax.all_to_all(parts, 'member', 0, 0, axis_index_groups=cores)  11.4 us
    all_to_all x1, waiting for transfers between devices, shards(): parts = lax.all_to_all(parts, 'member', 0, 0, axis_index_groups=cores)  6.34 us
    all_to_all x1, starting transfers between devices, shards(): cut = lax.all_to_all(cut.reshape(groups, -1, 8, LANES), 'group', 0, 0)  5.67 us
    all_to_all x1, waiting for transfers between devices, shards(): partner = lax.all_to_all(cut, 'group', 0, 0).reshape(high, wide, 8, LANES)  5.31 us
    pallas_call x1, Pallas kernels, run_head(): call(head_kernel, shape((8, dim, rows), F32), [SMEM, HBM, HBM, VMEM, VMEM...  4.69 us
    all_to_all x1, waiting for transfers between devices, shards(): cut = lax.all_to_all(cut.reshape(groups, -1, 8, LANES), 'group', 0, 0)  4.43 us
  transfers between devices with their start and end apart: 4, of which 4 were waited for; matrix products, arithmetic and copies ran while one was open for 0% of the time, Pallas kernels for 12%

profile of v1, /device:TPU:64, one launch (start us, length us, event | category | flops | bytes accessed | tf_op | source)
XLA Modules:
  0.0 90.8 jit_solution(6490148121368896800)
XLA Ops:
  0.6 0.0 copy-start.1
  0.6 5.7 %all-to-all-start = ((bf16[8,25,8,128]{3,2,1,0:T(8,128)(2,1)}), bf16[8,25,8,128]{3,2,1,0:T(8,128)(2,1)S(1)}, u32[]{:S(2)}, u32[]{:S(2)}) async-start(bf16[8,25,8,128]{3,2,1,0:T(8,128)(2,1)} %bitcast.19), calls=%async_computation | async-start | bytes 819200 | tf_op jit(solution)/shard_map/all_to_all | solution.py:377
  7.0 3.5 %shard_map.95.weights = f32[400,128]{1,0:T(8,128)} custom-call(s32[1,1]{1,0:T(1,128)S(6)} %copy.10.count, s32[16]{0:T(128)} %rel_ids.1, f32[400,2112]{1,0:T(8,128)} %bitcast.22), custom_call_target="tpu_custom_call" | custom-call | flops 2560000000 | bytes 3379200 | tf_op jit(solution)/shard_map/pallas_call | solution.py:287
  10.4 0.0 copy-start
  10.5 0.0 copy-start.2
  10.5 4.4 %all-to-all-done.rows = bf16[8,25,8,128]{3,2,1,0:T(8,128)(2,1)S(1)} async-done(((bf16[8,25,8,128]{3,2,1,0:T(8,128)(2,1)}), bf16[8,25,8,128]{3,2,1,0:T(8,128)(2,1)S(1)}, u32[]{:S(2)}, u32[]{:S(2)}) %all-to-all-start) | async-done | bytes 409632 | tf_op jit(solution)/shard_map/all_to_all | solution.py:377
  14.9 0.0 copy-done.1
  14.9 1.4 %shard_map.97 = bf16[8,25,8,128]{3,2,1,0:T(8,128)(2,1)} custom-call(s32[8]{0:T(128)S(1)} %copy-done.1, bf16[8,25,8,128]{3,2,1,0:T(8,128)(2,1)S(1)} %all-to-all-done.rows), custom_call_target="tpu_custom_call" | custom-call | bytes 819200 | tf_op jit(solution)/shard_map/pallas_call | solution.py:380
  16.3 3.5 %all-to-all-start.1 = ((bf16[8,25,8,128]{3,2,1,0:T(8,128)(2,1)}), bf16[8,25,8,128]{3,2,1,0:T(8,128)(2,1)S(1)}, u32[]{:S(2)}, u32[]{:S(2)}) async-start(bf16[8,25,8,128]{3,2,1,0:T(8,128)(2,1)} %shard_map.97), calls=%async_computation.1 | async-start | bytes 819200 | tf_op jit(solution)/shard_map/all_to_all | solution.py:383
  19.7 2.8 %shard_map.96.query = bf16[32,400,256]{2,1,0:T(8,128)(2,1)} custom-call(s32[1,1]{1,0:T(1,128)S(6)} %copy.10.count, bf16[400,512]{1,0:T(8,128)(2,1)} %bitcast.20, s32[16,256]{1,0:T(8,128)} %heads.3, f32[400,128]{1,0:T(8,128)} %shard_map.95.weights), custom_call_target="tpu_custom_call" | custom-call | flops 1677721600 | bytes 3276800 | tf_op jit(solution)/shard_map/pallas_call | solution.py:302
  22.5 5.3 %all-to-all-done.1 = bf16[8,25,8,128]{3,2,1,0:T(8,128)(2,1)S(1)} async-done(((bf16[8,25,8,128]{3,2,1,0:T(8,128)(2,1)}), bf16[8,25,8,128]{3,2,1,0:T(8,128)(2,1)S(1)}, u32[]{:S(2)}, u32[]{:S(2)}) %all-to-all-start.1) | async-done | bytes 409632 | tf_op jit(solution)/shard_map/all_to_all | solution.py:383
  27.8 0.0 copy-done
  27.8 0.0 copy-done.2
  27.8 4.0 %shard_map.98 = (bf16[16,400,512]{2,1,0:T(8,128)(2,1)}, bf16[48,256,256]{2,1,0:T(8,128)(2,1)}, bf16[8,56,640]{2,1,0:T(8,128)(2,1)S(1)}) custom-call(s32[1,1]{1,0:T(1,128)S(6)} %copy.10.count, bf16[32,400,256]{2,1,0:T(8,128)(2,1)} %shard_map.96.query, bf16[400,512]{1,0:T(8,128)(2,1)S(1)} %bitcast.16, bf16[400,128]{1,0:T(8,128)(2,1)S(1)} %bitcast.17, ...), custom_call_target="tpu_custom_call" | custom-call | flops 5872025600 | bytes 13107200 | tf_op jit(solution)/shard_map/pallas_call | solution.py:318
  31.9 18.3 %all_to_all.25.back = bf16[8,56,640]{2,1,0:T(8,128)(2,1)S(1)} all-to-all(bf16[8,56,640]{2,1,0:T(8,128)(2,1)S(1)} %get-tuple-element.18), channel_id=1, replica_groups=mesh['group'=8,'member'=32] {'group'}, dimensions={0} | all-to-all | bytes 1146880 | tf_op jit(solution)/shard_map/all_to_all | solution.py:388
  50.2 0.1 collective-permute-start
  50.3 1.2 %collective-permute-done = bf16[56,128]{1,0:T(8,128)(2,1)S(1)} collective-permute-done((bf16[56,128]{1,0:T(8,128)(2,1)S(1)}, bf16[56,128]{1,0:T(8,128)(2,1)S(1)}, u32[]{:S(2)}, u32[]{:S(2)}) %collective-permute-start) | collective-permute-done | bytes 14368 | tf_op jit(solution)/shard_map/ppermute | solution.py:391
  51.5 0.7 broadcast_in_dim.2
  52.2 11.4 %all-to-all-start.3 = ((bf16[16,56,128]{2,1,0:T(8,128)(2,1)}), bf16[16,56,128]{2,1,0:T(8,128)(2,1)S(1)}, u32[]{:S(2)}, u32[]{:S(2)}) async-start(bf16[16,56,128]{2,1,0:T(8,128)(2,1)} %broadcast_in_dim.2), calls=%async_computation.3 | async-start | bytes 458752 | tf_op jit(solution)/shard_map/all_to_all | solution.py:395
  63.6 4.7 %shard_map.99.base = f32[8,400,512]{2,1,0:T(8,128)} custom-call(s32[1,1]{1,0:T(1,128)S(6)} %copy.10.count, bf16[16,400,512]{2,1,0:T(8,128)(2,1)} %get-tuple-element.22.pick, bf16[48,256,256]{2,1,0:T(8,128)(2,1)} %get-tuple-element.23.diff, f32[400,128]{1,0:T(8,128)} %shard_map.95.weights, s32[16,256]{1,0:T(8,128)} %heads.3, bf16[400,512]{1,0:T(8,128)(2,1)} %bitcast.21), custom_call_target="tpu_custom_call" | custom-call | flops 2516582400 | bytes 9830400 | tf_op jit(solution)/shard_map/pallas_call | solution.py:348
  68.3 6.3 %all-to-all-done.3.hub = bf16[16,56,128]{2,1,0:T(8,128)(2,1)S(1)} async-done(((bf16[16,56,128]{2,1,0:T(8,128)(2,1)}), bf16[16,56,128]{2,1,0:T(8,128)(2,1)S(1)}, u32[]{:S(2)}, u32[]{:S(2)}) %all-to-all-start.3) | async-done | bytes 229408 | tf_op jit(solution)/shard_map/all_to_all | solution.py:395
  74.7 1.7 %shard_map.100 = (bf16[8,56,640]{2,1,0:T(8,128)(2,1)S(1)}, f32[400,512]{1,0:T(8,128)S(1)}) custom-call(s32[8]{0:T(128)S(1)} %copy-done.1, bf16[8,56,640]{2,1,0:T(8,128)(2,1)S(1)} %all_to_all.25.back, bf16[16,56,128]{2,1,0:T(8,128)(2,1)S(1)} %all-to-all-done.3.hub, f32[8,400,512]{2,1,0:T(8,128)} %shard_map.99.base), custom_call_target="tpu_custom_call" | custom-call | bytes 1146880 | tf_op jit(solution)/shard_map/pallas_call | solution.py:398
  76.4 13.5 %all_to_all.26.last = bf16[8,56,640]{2,1,0:T(8,128)(2,1)S(1)} all-to-all(bf16[8,56,640]{2,1,0:T(8,128)(2,1)S(1)} %get-tuple-element.27), channel_id=1, replica_groups=mesh['group'=8,'member'=32] {'group'}, dimensions={0} | all-to-all | bytes 1146880 | tf_op jit(solution)/shard_map/all_to_all | solution.py:408
  89.9 0.9 shard_map.101
  (2 shorter events, 0.0 us)
Async XLA Ops:
  0.6 14.3 %copy-start.1 = (s32[8]{0:T(128)S(1)}, s32[8]{0:T(128)}, u32[]{:S(2)}) copy-start(s32[8]{0:T(128)} %matching.3) | copy-start | bytes 100
  0.6 14.3 %all-to-all-start = ((bf16[8,25,8,128]{3,2,1,0:T(8,128)(2,1)}), bf16[8,25,8,128]{3,2,1,0:T(8,128)(2,1)S(1)}, u32[]{:S(2)}, u32[]{:S(2)}) async-start(bf16[8,25,8,128]{3,2,1,0:T(8,128)(2,1)} %bitcast.19), calls=%async_computation | async-start | bytes 819200 | tf_op jit(solution)/shard_map/all_to_all | solution.py:377
  10.4 17.4 %copy-start = (bf16[128,400]{0,1:T(8,128)(2,1)S(1)}, bf16[128,400]{0,1:T(8,128)(2,1)}, u32[]{:S(2)}) copy-start(bf16[128,400]{0,1:T(8,128)(2,1)} %param.9) | copy-start | bytes 307204
  10.5 17.4 %copy-start.2 = (s32[16,256]{1,0:T(8,128)S(1)}, s32[16,256]{1,0:T(8,128)}, u32[]{:S(2)}) copy-start(s32[16,256]{1,0:T(8,128)} %tails.1) | copy-start | bytes 49156
  16.3 11.6 %all-to-all-start.1 = ((bf16[8,25,8,128]{3,2,1,0:T(8,128)(2,1)}), bf16[8,25,8,128]{3,2,1,0:T(8,128)(2,1)S(1)}, u32[]{:S(2)}, u32[]{:S(2)}) async-start(bf16[8,25,8,128]{3,2,1,0:T(8,128)(2,1)} %shard_map.97), calls=%async_computation.1 | async-start | bytes 819200 | tf_op jit(solution)/shard_map/all_to_all | solution.py:383
  50.2 1.3 %collective-permute-start = (bf16[56,128]{1,0:T(8,128)(2,1)S(1)}, bf16[56,128]{1,0:T(8,128)(2,1)S(1)}, u32[]{:S(2)}, u32[]{:S(2)}) collective-permute-start(bf16[56,128]{1,0:T(8,128)(2,1)S(1)} %slice_reduce_fusion), channel_id=1, source_target_pairs={{0,1},{1,0},{2,3},{3,2},{4,5},{5,4},{6,7},{7,6},{8,9},{9,8},{10,11... | collective-permute-start | bytes 43016 | tf_op jit(solution)/shard_map/ppermute | solution.py:391
  52.2 22.5 %all-to-all-start.3 = ((bf16[16,56,128]{2,1,0:T(8,128)(2,1)}), bf16[16,56,128]{2,1,0:T(8,128)(2,1)S(1)}, u32[]{:S(2)}, u32[]{:S(2)}) async-start(bf16[16,56,128]{2,1,0:T(8,128)(2,1)} %broadcast_in_dim.2), calls=%async_computation.3 | async-start | bytes 458752 | tf_op jit(solution)/shard_map/all_to_all | solution.py:395

commit v2 on v1

--- a/solution.py
+++ b/solution.py
@@ -16,8 +16,8 @@
 
 
 def hot(ids, rows):
-    row = lax.broadcasted_iota(jnp.int32, (rows, ids.shape[1]), 0)
-    return jnp.where(row == ids, 1.0, 0.0).astype(BF)
+    row = lax.broadcasted_iota(jnp.int32, (rows, ids.shape[1]), 0).astype(jnp.int16)
+    return jnp.where(row == ids.astype(jnp.int16), jnp.ones((), BF), jnp.zeros((), BF))
 
 
 def pair_ids(ids_ref, pair):
@@ -90,6 +90,20 @@
     @pl.loop(0, pairs)
     def _(pair):
         put(pair).wait()
+
+
+def sizes(dim, rows, hubs, chunks):
+    return dim // 8 * (rows // LANES) // chunks, -(-(dim // 8 * (hubs // LANES)) // chunks)
+
+
+def places(dim, rows, hubs, chunks):
+    own, more = sizes(dim, rows, hubs, chunks)
+    found = []
+    for first, base, width, each in ((0, 0, rows, own), (own, rows, hubs, more)):
+        wide = width // LANES
+        for t in range(dim // 8 * wide):
+            found.append((t // each, first + t % each, t // wide * 8, base + t % wide * LANES))
+    return found
 
 
 def tail_kernel(count, query, partner, hub, tails, pick, diff, grads, table, acc, qin, picks, diffs, moves, qsem, psem, dsem):
@@ -166,12 +180,10 @@
                 put_pick(pair + 1, 1 - slot).start()
 
     spread(pairs - 1, 1)
-    chunks, step = grads.shape[0], grads.shape[1]
-    for c in range(chunks):
-        n = min(step, dim - c * step)
-        grads[c, :n] = acc[c * step : c * step + n].astype(BF)
-        if n < step:
-            grads[c, n:] = jnp.zeros((step - n, grads.shape[2]), BF)
+    for chunk, at, row, lane in places(dim, rows, hub.shape[1], grads.shape[0]):
+        grads[chunk, at] = acc[row : row + 8, lane : lane + LANES].astype(BF)
+    for at in range(at + 1, grads.shape[1]):
+        grads[chunk, at] = jnp.zeros((8, LANES), BF)
     put_pick(pairs - 1, 1).wait()
 
     @pl.loop(0, pairs)
@@ -228,10 +240,6 @@
     put.wait()
 
 
-def parts_of(dim, step):
-    return [(at, min(step, dim - at)) for at in range(0, dim, step)]
-
-
 def reorder_kernel(matching, rows, out, sems):
     puts = [
         pltpu.make_async_copy(rows.at[matching[g]], out.at[g], sems.at[g]) for g in range(out.shape[0])
@@ -242,27 +250,43 @@
         put.wait()
 
 
-def return_kernel(matching, back, hub, base, out, held, sem):
-    load = pltpu.make_async_copy(base.at[0], held, sem)
-    load.start()
-    rows = out.shape[2] - hub.shape[2]
+def return_kernel(matching, back, hub, out):
+    own = out.shape[1] - hub.shape[1]
     total = hub[0].astype(F32)
     for m in range(1, hub.shape[0]):
         total += hub[m].astype(F32)
     total = total.astype(BF)
     for g in range(out.shape[0]):
-        out[matching[g], :, :rows] = back[g, :, :rows]
-        out[g, :, rows:] = total
-    load.wait()
-
-
-def update_kernel(base, hub, last, new_ent, new_hub):
-    dim, rows = base.shape
-    for i, (at, n) in enumerate(parts_of(dim, last.shape[1])):
-        rng = slice(at, at + n)
-        got = last[i, :n].astype(F32)
-        new_ent[rng] = (base[rng] - learn_rate * got[:, :rows]).astype(BF)
-        new_hub[rng] = (hub[rng].astype(F32) - learn_rate * got[:, rows:]).astype(BF)
+        out[matching[g], :own] = back[g, :own]
+        out[g, own:] = total
+
+
+def update_kernel(base, hub, last, new_ent, new_hub, held, sems):
+    dim, rows = new_ent.shape
+    step = 80
+    loads = [
+        pltpu.make_async_copy(base.at[0, pl.ds(at, step)], held.at[pl.ds(at, step)], sems.at[i])
+        for i, at in enumerate(range(0, dim, step))
+    ]
+    for load in loads:
+        load.start()
+    where = {(row, lane): (chunk, at) for chunk, at, row, lane in places(dim, rows, hub.shape[1], last.shape[0])}
+
+    def got(row, lane):
+        return jnp.concatenate([last[where[row, lane]], last[where[row + 8, lane]]], axis=0).astype(F32)
+
+    for row in range(0, dim, 16):
+        at = slice(row, row + 16)
+        for lane in range(0, hub.shape[1], LANES):
+            to = slice(lane, lane + LANES)
+            new_hub[at, to] = (hub[at, to].astype(F32) - learn_rate * got(row, rows + lane)).astype(BF)
+    for row in range(0, dim, 16):
+        if row % step == 0:
+            loads[row // step].wait()
+        at = slice(row, row + 16)
+        for lane in range(0, rows, LANES):
+            to = slice(lane, lane + LANES)
+            new_ent[at, to] = (held[at, to] - learn_rate * got(row, lane)).astype(BF)
 
 
 def call(kernel, out_shape, in_specs, out_specs, flops, moved, scratch=(), exps=0, vmem=32, aliases={}):
@@ -311,7 +335,7 @@
     )(tile_count, ent, head_index, weights)
 
 
-def run_tail(tile_count, query, partner, hub, tail_index, groups, step):
+def run_tail(tile_count, query, partner, hub, tail_index, groups):
     tiles, edges = tail_index.shape
     dim = query.shape[1]
     rows, hubs = partner.shape[1], hub.shape[1]
@@ -320,7 +344,7 @@
         [
             shape((tiles, dim, 2 * edges), BF),
             shape((3 * tiles, edges, edges), BF),
-            shape((groups, step, rows + hubs), BF),
+            shape((groups, sum(sizes(dim, rows, hubs, groups)), 8, LANES), BF),
         ],
         [SMEM, HBM, VMEM, VMEM, VMEM],
         [HBM, HBM, VMEM],
@@ -370,7 +394,7 @@
         ent, hub, rel = entities.T, hub_rows.T, relations.T
         dim, rows = ent.shape
         hubs = hub.shape[1]
-        step = -(-dim // (8 * groups)) * 8
+        own = sizes(dim, rows, hubs, groups)[0]
 
         high, wide = dim // 8, rows // LANES
         cut = ent.reshape(high, 8, wide, LANES).transpose(0, 2, 1, 3)
@@ -383,11 +407,11 @@
         partner = lax.all_to_all(cut, "group", 0, 0).reshape(high, wide, 8, LANES)
         partner = partner.transpose(0, 2, 1, 3).reshape(dim, rows)
         query = run_query(tile_count, ent, head_index, weights)
-        pick, diff, grads = run_tail(tile_count, query, partner, hub, tail_index, groups, step)
+        pick, diff, grads = run_tail(tile_count, query, partner, hub, tail_index, groups)
 
         got = lax.all_to_all(grads, "group", 0, 0)
         got, pick, diff = lax.optimization_barrier((got, pick, diff))
-        part = jnp.sum(got[:, :, rows:].astype(F32), axis=0).astype(BF)
+        part = jnp.sum(got[:, own:].astype(F32), axis=0).astype(BF)
         other = lax.ppermute(part, "member", [(m, m ^ 1) for m in range(members)])
         part = (part.astype(F32) + other.astype(F32)).astype(BF)
         cores = [list(range(core, members, 2)) for core in range(2)]
@@ -395,24 +419,19 @@
         parts = lax.all_to_all(parts, "member", 0, 0, axis_index_groups=cores)
         base = run_head(tile_count, pick, diff, weights, head_index, ent)
         parts, base = lax.optimization_barrier((parts, base))
-        sent, base = call(
-            return_kernel,
-            [shape(got.shape, BF), shape((dim, rows), F32)],
-            [SMEM, VMEM, VMEM, HBM],
-            [VMEM, VMEM],
-            0,
-            4 * got.size,
-            [DMA(())],
-            vmem=50,
-        )(matching, got, parts, base)
+        sent = call(
+            return_kernel, shape(got.shape, BF), [SMEM, VMEM, VMEM], VMEM, 0, 4 * got.size
+        )(matching, got, parts)
         last = lax.all_to_all(sent, "group", 0, 0)
         new_ent, new_hub = call(
             update_kernel,
             [shape((dim, rows), BF), shape((dim, hubs), BF)],
-            [VMEM, VMEM, VMEM],
+            [HBM, VMEM, VMEM],
             [VMEM, VMEM],
             0,
             8 * dim * rows,
+            [pltpu.VMEM((dim, rows), F32), DMA((5,))],
+            vmem=50,
         )(base, hub, last)
         return (new_ent.T, new_hub.T)
 

time: 91.2 us -> 88.9 us (0.975)
  starting transfers between devices: 20.7 us -> 18.2 us
    all_to_all x1, starting transfers between devices: 11.4 us -> 8.96 us  [shards(): parts = lax.all_to_all(parts, 'member', 0, 0, axis_index_groups=cores)]
where the time goes in v2:
time: 88.9 us; the launch traced here: 88.3 us
  blocking collectives  31.7 us (36%)
  Pallas kernels  18.9 us (21%)
  starting transfers between devices  18.2 us (20%)
  waiting for transfers between devices  17.3 us (19%)
  between operations  1.38 us (2%)
    all_to_all x1, blocking collectives, shards(): got = lax.all_to_all(grads, 'group', 0, 0)  19 us
    all_to_all x1, blocking collectives, shards(): last = lax.all_to_all(sent, 'group', 0, 0)  12.7 us
    all_to_all x1, starting transfers between devices, shards(): parts = lax.all_to_all(parts, 'member', 0, 0, axis_index_groups=cores)  8.96 us
    all_to_all x1, waiting for transfers between devices, shards(): parts = lax.all_to_all(parts, 'member', 0, 0, axis_index_groups=cores)  6.45 us
    all_to_all x1, starting transfers between devices, shards(): cut = lax.all_to_all(cut.reshape(groups, -1, 8, LANES), 'group', 0, 0)  5.67 us
    all_to_all x1, waiting for transfers between devices, shards(): partner = lax.all_to_all(cut, 'group', 0, 0).reshape(high, wide, 8, LANES)  5.31 us
    pallas_call x1, Pallas kernels, run_head(): call(head_kernel, shape((8, dim, rows), F32), [SMEM, HBM, HBM, VMEM, VMEM...  4.65 us
    all_to_all x1, waiting for transfers between devices, shards(): cut = lax.all_to_all(cut.reshape(groups, -1, 8, LANES), 'group', 0, 0)  4.42 us
  transfers between devices with their start and end apart: 4, of which 4 were waited for; matrix products, arithmetic and copies ran while one was open for 0% of the time, Pallas kernels for 12%

profile of v2, /device:TPU:64, one launch (start us, length us, event | category | flops | bytes accessed | tf_op | source)
XLA Modules:
  0.0 88.3 jit_solution(12699786811883819143)
XLA Ops:
  0.6 0.0 copy-start.1
  0.6 5.7 %all-to-all-start = ((bf16[8,25,8,128]{3,2,1,0:T(8,128)(2,1)}), bf16[8,25,8,128]{3,2,1,0:T(8,128)(2,1)S(1)}, u32[]{:S(2)}, u32[]{:S(2)}) async-start(bf16[8,25,8,128]{3,2,1,0:T(8,128)(2,1)} %bitcast.19), calls=%async_computation | async-start | bytes 819200 | tf_op jit(solution)/shard_map/all_to_all | solution.py:401
  7.0 3.5 %shard_map.95.weights = f32[400,128]{1,0:T(8,128)} custom-call(s32[1,1]{1,0:T(1,128)S(6)} %copy.10.count, s32[16]{0:T(128)} %rel_ids.1, f32[400,2112]{1,0:T(8,128)} %bitcast.22), custom_call_target="tpu_custom_call" | custom-call | flops 2560000000 | bytes 3379200 | tf_op jit(solution)/shard_map/pallas_call | solution.py:311
  10.5 0.0 copy-start
  10.5 0.0 copy-start.2
  10.5 4.4 %all-to-all-done.rows = bf16[8,25,8,128]{3,2,1,0:T(8,128)(2,1)S(1)} async-done(((bf16[8,25,8,128]{3,2,1,0:T(8,128)(2,1)}), bf16[8,25,8,128]{3,2,1,0:T(8,128)(2,1)S(1)}, u32[]{:S(2)}, u32[]{:S(2)}) %all-to-all-start) | async-done | bytes 409632 | tf_op jit(solution)/shard_map/all_to_all | solution.py:401
  14.9 0.0 copy-done.1
  14.9 1.4 %shard_map.97 = bf16[8,25,8,128]{3,2,1,0:T(8,128)(2,1)} custom-call(s32[8]{0:T(128)S(1)} %copy-done.1, bf16[8,25,8,128]{3,2,1,0:T(8,128)(2,1)S(1)} %all-to-all-done.rows), custom_call_target="tpu_custom_call" | custom-call | bytes 819200 | tf_op jit(solution)/shard_map/pallas_call | solution.py:404
  16.3 3.5 %all-to-all-start.1 = ((bf16[8,25,8,128]{3,2,1,0:T(8,128)(2,1)}), bf16[8,25,8,128]{3,2,1,0:T(8,128)(2,1)S(1)}, u32[]{:S(2)}, u32[]{:S(2)}) async-start(bf16[8,25,8,128]{3,2,1,0:T(8,128)(2,1)} %shard_map.97), calls=%async_computation.1 | async-start | bytes 819200 | tf_op jit(solution)/shard_map/all_to_all | solution.py:407
  19.7 2.8 %shard_map.96.query = bf16[32,400,256]{2,1,0:T(8,128)(2,1)} custom-call(s32[1,1]{1,0:T(1,128)S(6)} %copy.10.count, bf16[400,512]{1,0:T(8,128)(2,1)} %bitcast.20, s32[16,256]{1,0:T(8,128)} %heads.3, f32[400,128]{1,0:T(8,128)} %shard_map.95.weights), custom_call_target="tpu_custom_call" | custom-call | flops 1677721600 | bytes 3276800 | tf_op jit(solution)/shard_map/pallas_call | solution.py:326
  22.5 5.3 %all-to-all-done.1 = bf16[8,25,8,128]{3,2,1,0:T(8,128)(2,1)S(1)} async-done(((bf16[8,25,8,128]{3,2,1,0:T(8,128)(2,1)}), bf16[8,25,8,128]{3,2,1,0:T(8,128)(2,1)S(1)}, u32[]{:S(2)}, u32[]{:S(2)}) %all-to-all-start.1) | async-done | bytes 409632 | tf_op jit(solution)/shard_map/all_to_all | solution.py:407
  27.8 0.0 copy-done
  27.8 0.0 copy-done.2
  27.8 3.9 %shard_map.98 = (bf16[16,400,512]{2,1,0:T(8,128)(2,1)}, bf16[48,256,256]{2,1,0:T(8,128)(2,1)}, bf16[8,32,8,128]{3,2,1,0:T(8,128)(2,1)S(1)}) custom-call(s32[1,1]{1,0:T(1,128)S(6)} %copy.10.count, bf16[32,400,256]{2,1,0:T(8,128)(2,1)} %shard_map.96.query, bf16[400,512]{1,0:T(8,128)(2,1)S(1)} %bitcast.16, bf16[400,128]{1,0:T(8,128)(2,1)S(1)} %bitcast.17, ...), custom_call_target="tpu_custom_call" | custom-call | flops 5872025600 | bytes 13107200 | tf_op jit(solution)/shard_map/pallas_call | solution.py:342
  31.8 19.0 %all_to_all.25.back = bf16[8,32,8,128]{3,2,1,0:T(8,128)(2,1)S(1)} all-to-all(bf16[8,32,8,128]{3,2,1,0:T(8,128)(2,1)S(1)} %get-tuple-element.16), channel_id=1, replica_groups=mesh['group'=8,'member'=32] {'group'}, dimensions={0} | all-to-all | bytes 1048576 | tf_op jit(solution)/shard_map/all_to_all | solution.py:412
  50.8 0.1 collective-permute-start
  50.9 1.2 %collective-permute-done = bf16[7,8,128]{2,1,0:T(8,128)(2,1)S(1)} collective-permute-done((bf16[7,8,128]{2,1,0:T(8,128)(2,1)S(1)}, bf16[7,8,128]{2,1,0:T(8,128)(2,1)S(1)}, u32[]{:S(2)}, u32[]{:S(2)}) %collective-permute-start) | collective-permute-done | bytes 14368 | tf_op jit(solution)/shard_map/ppermute | solution.py:415
  52.1 0.7 broadcast_in_dim.2
  52.8 9.0 %all-to-all-start.3 = ((bf16[16,7,8,128]{3,2,1,0:T(8,128)(2,1)}), bf16[16,7,8,128]{3,2,1,0:T(8,128)(2,1)S(1)}, u32[]{:S(2)}, u32[]{:S(2)}) async-start(bf16[16,7,8,128]{3,2,1,0:T(8,128)(2,1)} %broadcast_in_dim.2), calls=%async_computation.3 | async-start | bytes 458752 | tf_op jit(solution)/shard_map/all_to_all | solution.py:419
  61.8 4.6 %shard_map.99.base = f32[8,400,512]{2,1,0:T(8,128)} custom-call(s32[1,1]{1,0:T(1,128)S(6)} %copy.10.count, bf16[16,400,512]{2,1,0:T(8,128)(2,1)} %get-tuple-element.20.pick, bf16[48,256,256]{2,1,0:T(8,128)(2,1)} %get-tuple-element.21.diff, f32[400,128]{1,0:T(8,128)} %shard_map.95.weights, s32[16,256]{1,0:T(8,128)} %heads.3, bf16[400,512]{1,0:T(8,128)(2,1)} %bitcast.21), custom_call_target="tpu_custom_call" | custom-call | flops 2516582400 | bytes 9830400 | tf_op jit(solution)/shard_map/pallas_call | solution.py:372
  66.4 6.4 %all-to-all-done.3.hub = bf16[16,7,8,128]{3,2,1,0:T(8,128)(2,1)S(1)} async-done(((bf16[16,7,8,128]{3,2,1,0:T(8,128)(2,1)}), bf16[16,7,8,128]{3,2,1,0:T(8,128)(2,1)S(1)}, u32[]{:S(2)}, u32[]{:S(2)}) %all-to-all-start.3) | async-done | bytes 229408 | tf_op jit(solution)/shard_map/all_to_all | solution.py:419
  72.9 0.6 shard_map.100
  73.5 12.7 %all_to_all.26.last = bf16[8,32,8,128]{3,2,1,0:T(8,128)(2,1)S(1)} all-to-all(bf16[8,32,8,128]{3,2,1,0:T(8,128)(2,1)S(1)} %shard_map.100), channel_id=1, replica_groups=mesh['group'=8,'member'=32] {'group'}, dimensions={0} | all-to-all | bytes 1048576 | tf_op jit(solution)/shard_map/all_to_all | solution.py:425
  86.2 2.1 %shard_map.101 = (bf16[400,512]{1,0:T(8,128)(2,1)}, bf16[400,128]{1,0:T(8,128)(2,1)}) custom-call(f32[8,400,512]{2,1,0:T(8,128)} %shard_map.99.base, bf16[400,128]{1,0:T(8,128)(2,1)S(1)} %bitcast.18, bf16[8,32,8,128]{3,2,1,0:T(8,128)(2,1)S(1)} %all_to_all.26.last), custom_call_target="tpu_custom_call" | custom-call | bytes 1638400 | tf_op jit(solution)/shard_map/pallas_call | solution.py:426
  (2 shorter events, 0.0 us)
Async XLA Ops:
  0.6 14.3 %copy-start.1 = (s32[8]{0:T(128)S(1)}, s32[8]{0:T(128)}, u32[]{:S(2)}) copy-start(s32[8]{0:T(128)} %matching.3) | copy-start | bytes 100
  0.6 14.3 %all-to-all-start = ((bf16[8,25,8,128]{3,2,1,0:T(8,128)(2,1)}), bf16[8,25,8,128]{3,2,1,0:T(8,128)(2,1)S(1)}, u32[]{:S(2)}, u32[]{:S(2)}) async-start(bf16[8,25,8,128]{3,2,1,0:T(8,128)(2,1)} %bitcast.19), calls=%async_computation | async-start | bytes 819200 | tf_op jit(solution)/shard_map/all_to_all | solution.py:401
  10.5 17.4 %copy-start = (bf16[128,400]{0,1:T(8,128)(2,1)S(1)}, bf16[128,400]{0,1:T(8,128)(2,1)}, u32[]{:S(2)}) copy-start(bf16[128,400]{0,1:T(8,128)(2,1)} %param.9) | copy-start | bytes 307204
  10.5 17.4 %copy-start.2 = (s32[16,256]{1,0:T(8,128)S(1)}, s32[16,256]{1,0:T(8,128)}, u32[]{:S(2)}) copy-start(s32[16,256]{1,0:T(8,128)} %tails.1) | copy-start | bytes 49156
  16.3 11.6 %all-to-all-start.1 = ((bf16[8,25,8,128]{3,2,1,0:T(8,128)(2,1)}), bf16[8,25,8,128]{3,2,1,0:T(8,128)(2,1)S(1)}, u32[]{:S(2)}, u32[]{:S(2)}) async-start(bf16[8,25,8,128]{3,2,1,0:T(8,128)(2,1)} %shard_map.97), calls=%async_computation.1 | async-start | bytes 819200 | tf_op jit(solution)/shard_map/all_to_all | solution.py:407
  50.8 1.3 %collective-permute-start = (bf16[7,8,128]{2,1,0:T(8,128)(2,1)S(1)}, bf16[7,8,128]{2,1,0:T(8,128)(2,1)S(1)}, u32[]{:S(2)}, u32[]{:S(2)}) collective-permute-start(bf16[7,8,128]{2,1,0:T(8,128)(2,1)S(1)} %slice_reduce_fusion), channel_id=1, source_target_pairs={{0,1},{1,0},{2,3},{3,2},{4,5},{5,4},{6,7},{7,6},{8,9},{9,8},{10,11... | collective-permute-start | bytes 43016 | tf_op jit(solution)/shard_map/ppermute | solution.py:415
  52.8 20.1 %all-to-all-start.3 = ((bf16[16,7,8,128]{3,2,1,0:T(8,128)(2,1)}), bf16[16,7,8,128]{3,2,1,0:T(8,128)(2,1)S(1)}, u32[]{:S(2)}, u32[]{:S(2)}) async-start(bf16[16,7,8,128]{3,2,1,0:T(8,128)(2,1)} %broadcast_in_dim.2), calls=%async_computation.3 | async-start | bytes 458752 | tf_op jit(solution)/shard_map/all_to_all | solution.py:419

commit v3 on v2

--- a/solution.py
+++ b/solution.py
@@ -9,6 +9,8 @@
 BF = jnp.bfloat16
 F32 = jnp.float32
 LANES = 128
+STEP = 80
+HELD = 160
 VMEM = pl.BlockSpec(memory_space=pltpu.VMEM)
 SMEM = pl.BlockSpec(memory_space=pltpu.SMEM)
 HBM = pl.BlockSpec(memory_space=pltpu.HBM)
@@ -191,7 +193,7 @@
         put_diff(pair).wait()
 
 
-def head_kernel(count, pick, diff, weights, heads, ent, base, pin, din, moves, acc, psem, dsem, sem):
+def head_kernel(count, pick, diff, weights, heads, ent, base, pin, din, moves, acc, own, psem, dsem, own_sem, sems):
     half = acc.shape[0] // 2
     edges = heads.shape[1]
     live = count[0, 0]
@@ -210,6 +212,8 @@
         get_pick(pair).start()
         get_diff(pair).start()
 
+    get_own = pltpu.make_async_copy(ent, own, own_sem)
+    get_own.start()
     acc[...] = jnp.zeros_like(acc)
     moves[...] = jnp.zeros_like(moves)
 
@@ -234,10 +238,15 @@
                 ).astype(BF)
 
     spread(pairs - 1, 1)
-    acc[...] = ent[...].astype(F32) - learn_rate * acc[...]
-    put = pltpu.make_async_copy(acc, base.at[0], sem)
-    put.start()
-    put.wait()
+    get_own.wait()
+    puts = []
+    for i, at in enumerate(range(0, acc.shape[0], STEP)):
+        rng = slice(at, at + STEP)
+        acc[rng] = own[rng].astype(F32) - learn_rate * acc[rng]
+        puts.append(pltpu.make_async_copy(acc.at[pl.ds(at, STEP)], base.at[0, pl.ds(at, STEP)], sems.at[i]))
+        puts[i].start()
+    for put in puts:
+        put.wait()
 
 
 def reorder_kernel(matching, rows, out, sems):
@@ -250,7 +259,9 @@
         put.wait()
 
 
-def return_kernel(matching, back, hub, out):
+def return_kernel(matching, back, hub, base, out, held, sem):
+    load = pltpu.make_async_copy(base.at[0, pl.ds(0, HELD)], held, sem)
+    load.start()
     own = out.shape[1] - hub.shape[1]
     total = hub[0].astype(F32)
     for m in range(1, hub.shape[0]):
@@ -259,16 +270,18 @@
     for g in range(out.shape[0]):
         out[matching[g], :own] = back[g, :own]
         out[g, own:] = total
-
-
-def update_kernel(base, hub, last, new_ent, new_hub, held, sems):
-    dim, rows = new_ent.shape
-    step = 80
-    loads = [
-        pltpu.make_async_copy(base.at[0, pl.ds(at, step)], held.at[pl.ds(at, step)], sems.at[i])
-        for i, at in enumerate(range(0, dim, step))
-    ]
-    for load in loads:
+    load.wait()
+
+
+def update_kernel(base, held, hub, last, new_ent, new_hub, more, ent_out, hub_out, get_sems, put_sems, hub_sem):
+    dim, rows = ent_out.shape
+    loads = {
+        at: pltpu.make_async_copy(
+            base.at[0, pl.ds(at, STEP)], more.at[pl.ds(at - HELD, STEP)], get_sems.at[i]
+        )
+        for i, at in enumerate(range(HELD, dim, STEP))
+    }
+    for load in loads.values():
         load.start()
     where = {(row, lane): (chunk, at) for chunk, at, row, lane in places(dim, rows, hub.shape[1], last.shape[0])}
 
@@ -279,14 +292,24 @@
         at = slice(row, row + 16)
         for lane in range(0, hub.shape[1], LANES):
             to = slice(lane, lane + LANES)
-            new_hub[at, to] = (hub[at, to].astype(F32) - learn_rate * got(row, rows + lane)).astype(BF)
-    for row in range(0, dim, 16):
-        if row % step == 0:
-            loads[row // step].wait()
-        at = slice(row, row + 16)
-        for lane in range(0, rows, LANES):
-            to = slice(lane, lane + LANES)
-            new_ent[at, to] = (held[at, to] - learn_rate * got(row, lane)).astype(BF)
+            hub_out[at, to] = (hub[at, to].astype(F32) - learn_rate * got(row, rows + lane)).astype(BF)
+    put_hub = pltpu.make_async_copy(hub_out, new_hub, hub_sem)
+    put_hub.start()
+    puts = []
+    for i, first in enumerate(range(0, dim, STEP)):
+        if first in loads:
+            loads[first].wait()
+        for row in range(first, first + STEP, 16):
+            for lane in range(0, rows, LANES):
+                to = slice(lane, lane + LANES)
+                old = held[row : row + 16, to] if row < HELD else more[row - HELD : row - HELD + 16, to]
+                ent_out[row : row + 16, to] = (old - learn_rate * got(row, lane)).astype(BF)
+        rng = pl.ds(first, STEP)
+        puts.append(pltpu.make_async_copy(ent_out.at[rng], new_ent.at[rng], put_sems.at[i]))
+        puts[i].start()
+    for put in puts:
+        put.wait()
+    put_hub.wait()
 
 
 def call(kernel, out_shape, in_specs, out_specs, flops, moved, scratch=(), exps=0, vmem=32, aliases={}):
@@ -372,7 +395,7 @@
     return call(
         head_kernel,
         shape((8, dim, rows), F32),
-        [SMEM, HBM, HBM, VMEM, VMEM, VMEM],
+        [SMEM, HBM, HBM, VMEM, VMEM, HBM],
         HBM,
         2 * tiles * edges * dim * (rows + edges),
         6 * tiles * dim * edges,
@@ -381,9 +404,11 @@
             pltpu.VMEM((tiles, edges, edges), BF),
             pltpu.VMEM((2, dim, 2 * edges), BF),
             pltpu.VMEM((dim, rows), F32),
+            pltpu.VMEM((dim, rows), BF),
             DMA((tiles // 2,)),
             DMA((tiles // 2,)),
             DMA(()),
+            DMA((dim // STEP,)),
         ],
         vmem=60,
     )(tile_count, pick, diff, weights, head_index, ent)
@@ -419,20 +444,34 @@
         parts = lax.all_to_all(parts, "member", 0, 0, axis_index_groups=cores)
         base = run_head(tile_count, pick, diff, weights, head_index, ent)
         parts, base = lax.optimization_barrier((parts, base))
-        sent = call(
-            return_kernel, shape(got.shape, BF), [SMEM, VMEM, VMEM], VMEM, 0, 4 * got.size
-        )(matching, got, parts)
+        sent, held = call(
+            return_kernel,
+            [shape(got.shape, BF), shape((HELD, rows), F32)],
+            [SMEM, VMEM, VMEM, HBM],
+            [VMEM, VMEM],
+            0,
+            4 * got.size,
+            [DMA(())],
+            vmem=50,
+        )(matching, got, parts, base)
         last = lax.all_to_all(sent, "group", 0, 0)
         new_ent, new_hub = call(
             update_kernel,
             [shape((dim, rows), BF), shape((dim, hubs), BF)],
-            [HBM, VMEM, VMEM],
-            [VMEM, VMEM],
+            [HBM, VMEM, VMEM, VMEM],
+            [HBM, HBM],
             0,
             8 * dim * rows,
-            [pltpu.VMEM((dim, rows), F32), DMA((5,))],
+            [
+                pltpu.VMEM((dim - HELD, rows), F32),
+                pltpu.VMEM((dim, rows), BF),
+                pltpu.VMEM((dim, hubs), BF),
+                DMA(((dim - HELD) // STEP,)),
+                DMA((dim // STEP,)),
+                DMA(()),
+            ],
             vmem=50,
-        )(base, hub, last)
+        )(base, held, hub, last)
         return (new_ent.T, new_hub.T)
 
     return shards

time: 88.9 us -> 89.8 us (1.010)
    pallas_call x1, Pallas kernels: 0.61 us -> 1.52 us  [shards(): call(return_kernel, [shape(got.shape, BF), shape((HELD, rows), F32)], [SM...]
where the time goes in v3:
time: 89.8 us; the launch traced here: 88.9 us
  blocking collectives  30.9 us (34%)
  Pallas kernels  19.5 us (22%)
  starting transfers between devices  18.9 us (21%)
  waiting for transfers between devices  17.5 us (19%)
  between operations  1.38 us (2%)
    all_to_all x1, blocking collectives, shards(): got = lax.all_to_all(grads, 'group', 0, 0)  18.1 us
    all_to_all x1, blocking collectives, shards(): last = lax.all_to_all(sent, 'group', 0, 0)  12.7 us
    all_to_all x1, starting transfers between devices, shards(): parts = lax.all_to_all(parts, 'member', 0, 0, axis_index_groups=cores)  9.69 us
    all_to_all x1, waiting for transfers between devices, shards(): parts = lax.all_to_all(parts, 'member', 0, 0, axis_index_groups=cores)  6.58 us
    all_to_all x1, starting transfers between devices, shards(): cut = lax.all_to_all(cut.reshape(groups, -1, 8, LANES), 'group', 0, 0)  5.67 us
    all_to_all x1, waiting for transfers between devices, shards(): partner = lax.all_to_all(cut, 'group', 0, 0).reshape(high, wide, 8, LANES)  5.31 us
    pallas_call x1, Pallas kernels, run_head(): call(head_kernel, shape((8, dim, rows), F32), [SMEM, HBM, HBM, VMEM, VMEM...  4.51 us
    all_to_all x1, waiting for transfers between devices, shards(): cut = lax.all_to_all(cut.reshape(groups, -1, 8, LANES), 'group', 0, 0)  4.43 us
  transfers between devices with their start and end apart: 4, of which 4 were waited for; matrix products, arithmetic and copies ran while one was open for 0% of the time, Pallas kernels for 12%

profile of v3, /device:TPU:64, one launch (start us, length us, event | category | flops | bytes accessed | tf_op | source)
XLA Modules:
  0.0 88.9 jit_solution(10652640961717739291)
XLA Ops:
  0.6 0.0 copy-start.1
  0.6 5.7 %all-to-all-start = ((bf16[8,25,8,128]{3,2,1,0:T(8,128)(2,1)}), bf16[8,25,8,128]{3,2,1,0:T(8,128)(2,1)S(1)}, u32[]{:S(2)}, u32[]{:S(2)}) async-start(bf16[8,25,8,128]{3,2,1,0:T(8,128)(2,1)} %bitcast.19), calls=%async_computation | async-start | bytes 819200 | tf_op jit(solution)/shard_map/all_to_all | solution.py:426
  7.0 3.5 %shard_map.95.weights = f32[400,128]{1,0:T(8,128)} custom-call(s32[1,1]{1,0:T(1,128)S(6)} %copy.10.count, s32[16]{0:T(128)} %rel_ids.1, f32[400,2112]{1,0:T(8,128)} %bitcast.22), custom_call_target="tpu_custom_call" | custom-call | flops 2560000000 | bytes 3379200 | tf_op jit(solution)/shard_map/pallas_call | solution.py:334
  10.4 0.0 copy-start
  10.5 0.0 copy-start.2
  10.5 4.4 %all-to-all-done.rows = bf16[8,25,8,128]{3,2,1,0:T(8,128)(2,1)S(1)} async-done(((bf16[8,25,8,128]{3,2,1,0:T(8,128)(2,1)}), bf16[8,25,8,128]{3,2,1,0:T(8,128)(2,1)S(1)}, u32[]{:S(2)}, u32[]{:S(2)}) %all-to-all-start) | async-done | bytes 409632 | tf_op jit(solution)/shard_map/all_to_all | solution.py:426
  14.9 0.0 copy-done.1
  14.9 1.4 %shard_map.97 = bf16[8,25,8,128]{3,2,1,0:T(8,128)(2,1)} custom-call(s32[8]{0:T(128)S(1)} %copy-done.1, bf16[8,25,8,128]{3,2,1,0:T(8,128)(2,1)S(1)} %all-to-all-done.rows), custom_call_target="tpu_custom_call" | custom-call | bytes 819200 | tf_op jit(solution)/shard_map/pallas_call | solution.py:429
  16.3 3.5 %all-to-all-start.1 = ((bf16[8,25,8,128]{3,2,1,0:T(8,128)(2,1)}), bf16[8,25,8,128]{3,2,1,0:T(8,128)(2,1)S(1)}, u32[]{:S(2)}, u32[]{:S(2)}) async-start(bf16[8,25,8,128]{3,2,1,0:T(8,128)(2,1)} %shard_map.97), calls=%async_computation.1 | async-start | bytes 819200 | tf_op jit(solution)/shard_map/all_to_all | solution.py:432
  19.7 2.8 %shard_map.96.query = bf16[32,400,256]{2,1,0:T(8,128)(2,1)} custom-call(s32[1,1]{1,0:T(1,128)S(6)} %copy.10.count, bf16[400,512]{1,0:T(8,128)(2,1)} %bitcast.20, s32[16,256]{1,0:T(8,128)} %heads.3, f32[400,128]{1,0:T(8,128)} %shard_map.95.weights), custom_call_target="tpu_custom_call" | custom-call | flops 1677721600 | bytes 3276800 | tf_op jit(solution)/shard_map/pallas_call | solution.py:349
  22.5 5.3 %all-to-all-done.1 = bf16[8,25,8,128]{3,2,1,0:T(8,128)(2,1)S(1)} async-done(((bf16[8,25,8,128]{3,2,1,0:T(8,128)(2,1)}), bf16[8,25,8,128]{3,2,1,0:T(8,128)(2,1)S(1)}, u32[]{:S(2)}, u32[]{:S(2)}) %all-to-all-start.1) | async-done | bytes 409632 | tf_op jit(solution)/shard_map/all_to_all | solution.py:432
  27.8 0.0 copy-done
  27.8 0.0 copy-done.2
  27.8 3.9 %shard_map.98 = (bf16[16,400,512]{2,1,0:T(8,128)(2,1)}, bf16[48,256,256]{2,1,0:T(8,128)(2,1)}, bf16[8,32,8,128]{3,2,1,0:T(8,128)(2,1)S(1)}) custom-call(s32[1,1]{1,0:T(1,128)S(6)} %copy.10.count, bf16[32,400,256]{2,1,0:T(8,128)(2,1)} %shard_map.96.query, bf16[400,512]{1,0:T(8,128)(2,1)S(1)} %bitcast.16, bf16[400,128]{1,0:T(8,128)(2,1)S(1)} %bitcast.17, ...), custom_call_target="tpu_custom_call" | custom-call | flops 5872025600 | bytes 13107200 | tf_op jit(solution)/shard_map/pallas_call | solution.py:365
  31.8 18.1 %all_to_all.25.back = bf16[8,32,8,128]{3,2,1,0:T(8,128)(2,1)S(1)} all-to-all(bf16[8,32,8,128]{3,2,1,0:T(8,128)(2,1)S(1)} %get-tuple-element.18), channel_id=1, replica_groups=mesh['group'=8,'member'=32] {'group'}, dimensions={0} | all-to-all | bytes 1048576 | tf_op jit(solution)/shard_map/all_to_all | solution.py:437
  49.9 0.1 collective-permute-start
  50.0 1.2 %collective-permute-done = bf16[7,8,128]{2,1,0:T(8,128)(2,1)S(1)} collective-permute-done((bf16[7,8,128]{2,1,0:T(8,128)(2,1)S(1)}, bf16[7,8,128]{2,1,0:T(8,128)(2,1)S(1)}, u32[]{:S(2)}, u32[]{:S(2)}) %collective-permute-start) | collective-permute-done | bytes 14368 | tf_op jit(solution)/shard_map/ppermute | solution.py:440
  51.2 0.7 broadcast_in_dim.2
  51.9 9.7 %all-to-all-start.3 = ((bf16[16,7,8,128]{3,2,1,0:T(8,128)(2,1)}), bf16[16,7,8,128]{3,2,1,0:T(8,128)(2,1)S(1)}, u32[]{:S(2)}, u32[]{:S(2)}) async-start(bf16[16,7,8,128]{3,2,1,0:T(8,128)(2,1)} %broadcast_in_dim.2), calls=%async_computation.3 | async-start | bytes 458752 | tf_op jit(solution)/shard_map/all_to_all | solution.py:444
  61.6 4.5 %shard_map.99.base = f32[8,400,512]{2,1,0:T(8,128)} custom-call(s32[1,1]{1,0:T(1,128)S(6)} %copy.10.count, bf16[16,400,512]{2,1,0:T(8,128)(2,1)} %get-tuple-element.22.pick, bf16[48,256,256]{2,1,0:T(8,128)(2,1)} %get-tuple-element.23.diff, f32[400,128]{1,0:T(8,128)} %shard_map.95.weights, s32[16,256]{1,0:T(8,128)} %heads.3, bf16[400,512]{1,0:T(8,128)(2,1)} %bitcast.21), custom_call_target="tpu_custom_call" | custom-call | flops 2516582400 | bytes 9830400 | tf_op jit(solution)/shard_map/pallas_call | solution.py:395
  66.1 6.6 %all-to-all-done.3.hub = bf16[16,7,8,128]{3,2,1,0:T(8,128)(2,1)S(1)} async-done(((bf16[16,7,8,128]{3,2,1,0:T(8,128)(2,1)}), bf16[16,7,8,128]{3,2,1,0:T(8,128)(2,1)S(1)}, u32[]{:S(2)}, u32[]{:S(2)}) %all-to-all-start.3) | async-done | bytes 229408 | tf_op jit(solution)/shard_map/all_to_all | solution.py:444
  72.7 1.5 %shard_map.100 = (bf16[8,32,8,128]{3,2,1,0:T(8,128)(2,1)S(1)}, f32[160,512]{1,0:T(8,128)S(1)}) custom-call(s32[8]{0:T(128)S(1)} %copy-done.1, bf16[8,32,8,128]{3,2,1,0:T(8,128)(2,1)S(1)} %all_to_all.25.back, bf16[16,7,8,128]{3,2,1,0:T(8,128)(2,1)S(1)} %all-to-all-done.3.hub, f32[8,400,512]{2,1,0:T(8,128)} %shard_map.99.base), custom_call_target="tpu_custom_call" | custom-call | bytes 1048576 | tf_op jit(solution)/shard_map/pallas_call | solution.py:447
  74.3 12.7 %all_to_all.26.last = bf16[8,32,8,128]{3,2,1,0:T(8,128)(2,1)S(1)} all-to-all(bf16[8,32,8,128]{3,2,1,0:T(8,128)(2,1)S(1)} %get-tuple-element.27), channel_id=1, replica_groups=mesh['group'=8,'member'=32] {'group'}, dimensions={0} | all-to-all | bytes 1048576 | tf_op jit(solution)/shard_map/all_to_all | solution.py:457
  87.0 1.9 %shard_map.101 = (bf16[400,512]{1,0:T(8,128)(2,1)}, bf16[400,128]{1,0:T(8,128)(2,1)}) custom-call(f32[8,400,512]{2,1,0:T(8,128)} %shard_map.99.base, f32[160,512]{1,0:T(8,128)S(1)} %get-tuple-element.26.held, bf16[400,128]{1,0:T(8,128)(2,1)S(1)} %bitcast.18, bf16[8,32,8,128]{3,2,1,0:T(8,128)(2,1)S(1)} %all_to_all.26.last), custom_call_target="tpu_custom_call" | custom-call | bytes 1638400 | tf_op jit(solution)/shard_map/pallas_call | solution.py:458
  (2 shorter events, 0.0 us)
Async XLA Ops:
  0.6 14.3 %copy-start.1 = (s32[8]{0:T(128)S(1)}, s32[8]{0:T(128)}, u32[]{:S(2)}) copy-start(s32[8]{0:T(128)} %matching.3) | copy-start | bytes 100
  0.6 14.3 %all-to-all-start = ((bf16[8,25,8,128]{3,2,1,0:T(8,128)(2,1)}), bf16[8,25,8,128]{3,2,1,0:T(8,128)(2,1)S(1)}, u32[]{:S(2)}, u32[]{:S(2)}) async-start(bf16[8,25,8,128]{3,2,1,0:T(8,128)(2,1)} %bitcast.19), calls=%async_computation | async-start | bytes 819200 | tf_op jit(solution)/shard_map/all_to_all | solution.py:426
  10.4 17.4 %copy-start = (bf16[128,400]{0,1:T(8,128)(2,1)S(1)}, bf16[128,400]{0,1:T(8,128)(2,1)}, u32[]{:S(2)}) copy-start(bf16[128,400]{0,1:T(8,128)(2,1)} %param.9) | copy-start | bytes 307204
  10.5 17.4 %copy-start.2 = (s32[16,256]{1,0:T(8,128)S(1)}, s32[16,256]{1,0:T(8,128)}, u32[]{:S(2)}) copy-start(s32[16,256]{1,0:T(8,128)} %tails.1) | copy-start | bytes 49156
  16.3 11.6 %all-to-all-start.1 = ((bf16[8,25,8,128]{3,2,1,0:T(8,128)(2,1)}), bf16[8,25,8,128]{3,2,1,0:T(8,128)(2,1)S(1)}, u32[]{:S(2)}, u32[]{:S(2)}) async-start(bf16[8,25,8,128]{3,2,1,0:T(8,128)(2,1)} %shard_map.97), calls=%async_computation.1 | async-start | bytes 819200 | tf_op jit(solution)/shard_map/all_to_all | solution.py:432
  49.9 1.3 %collective-permute-start = (bf16[7,8,128]{2,1,0:T(8,128)(2,1)S(1)}, bf16[7,8,128]{2,1,0:T(8,128)(2,1)S(1)}, u32[]{:S(2)}, u32[]{:S(2)}) collective-permute-start(bf16[7,8,128]{2,1,0:T(8,128)(2,1)S(1)} %slice_reduce_fusion), channel_id=1, source_target_pairs={{0,1},{1,0},{2,3},{3,2},{4,5},{5,4},{6,7},{7,6},{8,9},{9,8},{10,11... | collective-permute-start | bytes 43016 | tf_op jit(solution)/shard_map/ppermute | solution.py:440
  51.9 20.8 %all-to-all-start.3 = ((bf16[16,7,8,128]{3,2,1,0:T(8,128)(2,1)}), bf16[16,7,8,128]{3,2,1,0:T(8,128)(2,1)S(1)}, u32[]{:S(2)}, u32[]{:S(2)}) async-start(bf16[16,7,8,128]{3,2,1,0:T(8,128)(2,1)} %broadcast_in_dim.2), calls=%async_computation.3 | async-start | bytes 458752 | tf_op jit(solution)/shard_map/all_to_all | solution.py:444

commit v4 on v2

--- a/solution.py
+++ b/solution.py
@@ -191,7 +191,7 @@
         put_diff(pair).wait()
 
 
-def head_kernel(count, pick, diff, weights, heads, ent, base, pin, din, moves, acc, psem, dsem, sem):
+def head_kernel(count, pick, diff, weights, heads, ent, acc, pin, din, moves, own, psem, dsem, sem):
     half = acc.shape[0] // 2
     edges = heads.shape[1]
     live = count[0, 0]
@@ -210,6 +210,8 @@
         get_pick(pair).start()
         get_diff(pair).start()
 
+    get_own = pltpu.make_async_copy(ent, own, sem)
+    get_own.start()
     acc[...] = jnp.zeros_like(acc)
     moves[...] = jnp.zeros_like(moves)
 
@@ -234,10 +236,8 @@
                 ).astype(BF)
 
     spread(pairs - 1, 1)
-    acc[...] = ent[...].astype(F32) - learn_rate * acc[...]
-    put = pltpu.make_async_copy(acc, base.at[0], sem)
-    put.start()
-    put.wait()
+    get_own.wait()
+    acc[...] = own[...].astype(F32) - learn_rate * acc[...]
 
 
 def reorder_kernel(matching, rows, out, sems):
@@ -261,15 +261,8 @@
         out[g, own:] = total
 
 
-def update_kernel(base, hub, last, new_ent, new_hub, held, sems):
-    dim, rows = new_ent.shape
-    step = 80
-    loads = [
-        pltpu.make_async_copy(base.at[0, pl.ds(at, step)], held.at[pl.ds(at, step)], sems.at[i])
-        for i, at in enumerate(range(0, dim, step))
-    ]
-    for load in loads:
-        load.start()
+def update_kernel(base, hub, last, new_ent, new_hub):
+    dim, rows = base.shape
     where = {(row, lane): (chunk, at) for chunk, at, row, lane in places(dim, rows, hub.shape[1], last.shape[0])}
 
     def got(row, lane):
@@ -277,16 +270,12 @@
 
     for row in range(0, dim, 16):
         at = slice(row, row + 16)
+        for lane in range(0, rows, LANES):
+            to = slice(lane, lane + LANES)
+            new_ent[at, to] = (base[at, to] - learn_rate * got(row, lane)).astype(BF)
         for lane in range(0, hub.shape[1], LANES):
             to = slice(lane, lane + LANES)
             new_hub[at, to] = (hub[at, to].astype(F32) - learn_rate * got(row, rows + lane)).astype(BF)
-    for row in range(0, dim, 16):
-        if row % step == 0:
-            loads[row // step].wait()
-        at = slice(row, row + 16)
-        for lane in range(0, rows, LANES):
-            to = slice(lane, lane + LANES)
-            new_ent[at, to] = (held[at, to] - learn_rate * got(row, lane)).astype(BF)
 
 
 def call(kernel, out_shape, in_specs, out_specs, flops, moved, scratch=(), exps=0, vmem=32, aliases={}):
@@ -371,21 +360,21 @@
     dim, rows = ent.shape
     return call(
         head_kernel,
-        shape((8, dim, rows), F32),
-        [SMEM, HBM, HBM, VMEM, VMEM, VMEM],
-        HBM,
+        shape((dim, rows), F32),
+        [SMEM, HBM, HBM, VMEM, VMEM, HBM],
+        VMEM,
         2 * tiles * edges * dim * (rows + edges),
         6 * tiles * dim * edges,
         [
             pltpu.VMEM((tiles // 2, dim, 2 * edges), BF),
             pltpu.VMEM((tiles, edges, edges), BF),
             pltpu.VMEM((2, dim, 2 * edges), BF),
-            pltpu.VMEM((dim, rows), F32),
+            pltpu.VMEM((dim, rows), BF),
             DMA((tiles // 2,)),
             DMA((tiles // 2,)),
             DMA(()),
         ],
-        vmem=60,
+        vmem=50,
     )(tile_count, pick, diff, weights, head_index, ent)
 
 
@@ -426,12 +415,10 @@
         new_ent, new_hub = call(
             update_kernel,
             [shape((dim, rows), BF), shape((dim, hubs), BF)],
-            [HBM, VMEM, VMEM],
+            [VMEM, VMEM, VMEM],
             [VMEM, VMEM],
             0,
             8 * dim * rows,
-            [pltpu.VMEM((dim, rows), F32), DMA((5,))],
-            vmem=50,
         )(base, hub, last)
         return (new_ent.T, new_hub.T)
 

time: 88.9 us -> 88.2 us (level)
  the two profiles are of different devices: /device:TPU:64 before, /device:TPU:8 now
where the time goes in v4:
time: 88.2 us; the launch traced here: 87.4 us
  blocking collectives  28.1 us (32%)
  Pallas kernels  20.3 us (23%)
  starting transfers between devices  19.9 us (23%)
  waiting for transfers between devices  16.8 us (19%)
  between operations  1.41 us (2%)
    all_to_all x1, blocking collectives, shards(): got = lax.all_to_all(grads, 'group', 0, 0)  15.3 us
    all_to_all x1, blocking collectives, shards(): last = lax.all_to_all(sent, 'group', 0, 0)  12.8 us
    all_to_all x1, starting transfers between devices, shards(): parts = lax.all_to_all(parts, 'member', 0, 0, axis_index_groups=cores)  10.7 us
    all_to_all x1, waiting for transfers between devices, shards(): parts = lax.all_to_all(parts, 'member', 0, 0, axis_index_groups=cores)  7.15 us
    pallas_call x1, Pallas kernels, run_tail(): call(tail_kernel, [shape((tiles, dim, 2 * edges), BF), shape((3 * tiles,...  6.26 us
    all_to_all x1, starting transfers between devices, shards(): cut = lax.all_to_all(cut.reshape(groups, -1, 8, LANES), 'group', 0, 0)  5.67 us
    all_to_all x1, waiting for transfers between devices, shards(): partner = lax.all_to_all(cut, 'group', 0, 0).reshape(high, wide, 8, LANES)  4.43 us
    all_to_all x1, waiting for transfers between devices, shards(): cut = lax.all_to_all(cut.reshape(groups, -1, 8, LANES), 'group', 0, 0)  4.04 us
  transfers between devices with their start and end apart: 4, of which 4 were waited for; matrix products, arithmetic and copies ran while one was open for 0% of the time, Pallas kernels for 13%

profile of v4, /device:TPU:8, one launch (start us, length us, event | category | flops | bytes accessed | tf_op | source)
XLA Modules:
  0.0 87.4 jit_solution(3461609715639832050)
XLA Ops:
  0.6 0.0 copy-start.4
  0.6 5.7 %all-to-all-start = ((bf16[8,25,8,128]{3,2,1,0:T(8,128)(2,1)}), bf16[8,25,8,128]{3,2,1,0:T(8,128)(2,1)S(1)}, u32[]{:S(2)}, u32[]{:S(2)}) async-start(bf16[8,25,8,128]{3,2,1,0:T(8,128)(2,1)} %bitcast.16), calls=%async_computation | async-start | bytes 819200 | tf_op jit(solution)/shard_map/all_to_all | solution.py:390
  7.0 3.9 %shard_map.95.weights = f32[400,128]{1,0:T(8,128)} custom-call(s32[1,1]{1,0:T(1,128)S(6)} %copy.10.count, s32[16]{0:T(128)} %rel_ids.1, f32[400,2112]{1,0:T(8,128)} %bitcast.22), custom_call_target="tpu_custom_call" | custom-call | flops 2560000000 | bytes 3379200 | tf_op jit(solution)/shard_map/pallas_call | solution.py:300
  10.8 0.0 copy-start.2
  10.8 0.0 copy-start.5
  10.9 4.0 %all-to-all-done.rows = bf16[8,25,8,128]{3,2,1,0:T(8,128)(2,1)S(1)} async-done(((bf16[8,25,8,128]{3,2,1,0:T(8,128)(2,1)}), bf16[8,25,8,128]{3,2,1,0:T(8,128)(2,1)S(1)}, u32[]{:S(2)}, u32[]{:S(2)}) %all-to-all-start) | async-done | bytes 409632 | tf_op jit(solution)/shard_map/all_to_all | solution.py:390
  14.9 0.0 copy-done.4
  14.9 1.4 %shard_map.97 = bf16[8,25,8,128]{3,2,1,0:T(8,128)(2,1)} custom-call(s32[8]{0:T(128)S(1)} %copy-done.4, bf16[8,25,8,128]{3,2,1,0:T(8,128)(2,1)S(1)} %all-to-all-done.rows), custom_call_target="tpu_custom_call" | custom-call | bytes 819200 | tf_op jit(solution)/shard_map/pallas_call | solution.py:393
  16.3 3.5 %all-to-all-start.1 = ((bf16[8,25,8,128]{3,2,1,0:T(8,128)(2,1)}), bf16[8,25,8,128]{3,2,1,0:T(8,128)(2,1)S(1)}, u32[]{:S(2)}, u32[]{:S(2)}) async-start(bf16[8,25,8,128]{3,2,1,0:T(8,128)(2,1)} %shard_map.97), calls=%async_computation.1 | async-start | bytes 819200 | tf_op jit(solution)/shard_map/all_to_all | solution.py:396
  19.7 3.6 %shard_map.96.query = bf16[32,400,256]{2,1,0:T(8,128)(2,1)} custom-call(s32[1,1]{1,0:T(1,128)S(6)} %copy.10.count, bf16[400,512]{1,0:T(8,128)(2,1)} %bitcast.17, s32[16,256]{1,0:T(8,128)} %heads.3, f32[400,128]{1,0:T(8,128)} %shard_map.95.weights), custom_call_target="tpu_custom_call" | custom-call | flops 1677721600 | bytes 3276800 | tf_op jit(solution)/shard_map/pallas_call | solution.py:315
  23.4 4.4 %all-to-all-done.1 = bf16[8,25,8,128]{3,2,1,0:T(8,128)(2,1)S(1)} async-done(((bf16[8,25,8,128]{3,2,1,0:T(8,128)(2,1)}), bf16[8,25,8,128]{3,2,1,0:T(8,128)(2,1)S(1)}, u32[]{:S(2)}, u32[]{:S(2)}) %all-to-all-start.1) | async-done | bytes 409632 | tf_op jit(solution)/shard_map/all_to_all | solution.py:396
  27.8 0.0 copy-done.2
  27.8 0.0 copy-start.3
  27.9 6.3 %shard_map.98 = (bf16[16,400,512]{2,1,0:T(8,128)(2,1)}, bf16[48,256,256]{2,1,0:T(8,128)(2,1)}, bf16[8,32,8,128]{3,2,1,0:T(8,128)(2,1)S(1)}) custom-call(s32[1,1]{1,0:T(1,128)S(6)} %copy.10.count, bf16[32,400,256]{2,1,0:T(8,128)(2,1)} %shard_map.96.query, bf16[400,512]{1,0:T(8,128)(2,1)S(1)} %bitcast.19, bf16[400,128]{1,0:T(8,128)(2,1)S(1)} %bitcast.20, ...), custom_call_target="tpu_custom_call" | custom-call | flops 5872025600 | bytes 13107200 | tf_op jit(solution)/shard_map/pallas_call | solution.py:331
  34.1 15.3 %all_to_all.25.back = bf16[8,32,8,128]{3,2,1,0:T(8,128)(2,1)S(1)} all-to-all(bf16[8,32,8,128]{3,2,1,0:T(8,128)(2,1)S(1)} %get-tuple-element.16), channel_id=1, replica_groups=mesh['group'=8,'member'=32] {'group'}, dimensions={0} | all-to-all | bytes 1048576 | tf_op jit(solution)/shard_map/all_to_all | solution.py:401
  49.4 0.1 collective-permute-start
  49.5 1.2 %collective-permute-done = bf16[7,8,128]{2,1,0:T(8,128)(2,1)S(1)} collective-permute-done((bf16[7,8,128]{2,1,0:T(8,128)(2,1)S(1)}, bf16[7,8,128]{2,1,0:T(8,128)(2,1)S(1)}, u32[]{:S(2)}, u32[]{:S(2)}) %collective-permute-start) | collective-permute-done | bytes 14368 | tf_op jit(solution)/shard_map/ppermute | solution.py:404
  50.7 0.7 broadcast_in_dim.2
  51.4 10.7 %all-to-all-start.3 = ((bf16[16,7,8,128]{3,2,1,0:T(8,128)(2,1)}), bf16[16,7,8,128]{3,2,1,0:T(8,128)(2,1)S(1)}, u32[]{:S(2)}, u32[]{:S(2)}) async-start(bf16[16,7,8,128]{3,2,1,0:T(8,128)(2,1)} %broadcast_in_dim.2), calls=%async_computation.3 | async-start | bytes 458752 | tf_op jit(solution)/shard_map/all_to_all | solution.py:408
  62.1 3.7 %shard_map.99.base = f32[400,512]{1,0:T(8,128)S(1)} custom-call(s32[1,1]{1,0:T(1,128)S(6)} %copy.10.count, bf16[16,400,512]{2,1,0:T(8,128)(2,1)} %get-tuple-element.20.pick, bf16[48,256,256]{2,1,0:T(8,128)(2,1)} %get-tuple-element.21.diff, f32[400,128]{1,0:T(8,128)S(1)} %copy-done.1, s32[16,256]{1,0:T(8,128)S(1)} %copy-done.3, bf16[400,512]{1,0:T(8,128)(2,1)S(1)} %bitcast.18), custom_call_target="tpu_custom_call" | custom-call | flops 2516582400 | bytes 9830400 | tf_op jit(solution)/shard_map/pallas_call | solution.py:361
  65.8 7.1 %all-to-all-done.3.hub = bf16[16,7,8,128]{3,2,1,0:T(8,128)(2,1)S(1)} async-done(((bf16[16,7,8,128]{3,2,1,0:T(8,128)(2,1)}), bf16[16,7,8,128]{3,2,1,0:T(8,128)(2,1)S(1)}, u32[]{:S(2)}, u32[]{:S(2)}) %all-to-all-start.3) | async-done | bytes 229408 | tf_op jit(solution)/shard_map/all_to_all | solution.py:408
  73.0 0.6 shard_map.100
  73.6 12.8 %all_to_all.26.last = bf16[8,32,8,128]{3,2,1,0:T(8,128)(2,1)S(1)} all-to-all(bf16[8,32,8,128]{3,2,1,0:T(8,128)(2,1)S(1)} %shard_map.100), channel_id=1, replica_groups=mesh['group'=8,'member'=32] {'group'}, dimensions={0} | all-to-all | bytes 1048576 | tf_op jit(solution)/shard_map/all_to_all | solution.py:414
  86.4 0.9 %shard_map.101 = (bf16[400,512]{1,0:T(8,128)(2,1)}, bf16[400,128]{1,0:T(8,128)(2,1)}) custom-call(f32[400,512]{1,0:T(8,128)S(1)} %shard_map.99.base, bf16[400,128]{1,0:T(8,128)(2,1)S(1)} %bitcast.21, bf16[8,32,8,128]{3,2,1,0:T(8,128)(2,1)S(1)} %all_to_all.26.last), custom_call_target="tpu_custom_call" | custom-call | bytes 1638400 | tf_op jit(solution)/shard_map/pallas_call | solution.py:415
  (8 shorter events, 0.0 us)
Async XLA Ops:
  0.6 14.3 %copy-start.4 = (s32[8]{0:T(128)S(1)}, s32[8]{0:T(128)}, u32[]{:S(2)}) copy-start(s32[8]{0:T(128)} %matching.3) | copy-start | bytes 100
  0.6 14.3 %all-to-all-start = ((bf16[8,25,8,128]{3,2,1,0:T(8,128)(2,1)}), bf16[8,25,8,128]{3,2,1,0:T(8,128)(2,1)S(1)}, u32[]{:S(2)}, u32[]{:S(2)}) async-start(bf16[8,25,8,128]{3,2,1,0:T(8,128)(2,1)} %bitcast.16), calls=%async_computation | async-start | bytes 819200 | tf_op jit(solution)/shard_map/all_to_all | solution.py:390
  10.8 17.0 %copy-start.2 = (bf16[128,400]{0,1:T(8,128)(2,1)S(1)}, bf16[128,400]{0,1:T(8,128)(2,1)}, u32[]{:S(2)}) copy-start(bf16[128,400]{0,1:T(8,128)(2,1)} %param.9) | copy-start | bytes 307204
  10.8 17.0 %copy-start.5 = (s32[16,256]{1,0:T(8,128)S(1)}, s32[16,256]{1,0:T(8,128)}, u32[]{:S(2)}) copy-start(s32[16,256]{1,0:T(8,128)} %tails.1) | copy-start | bytes 49156
  16.3 11.6 %all-to-all-start.1 = ((bf16[8,25,8,128]{3,2,1,0:T(8,128)(2,1)}), bf16[8,25,8,128]{3,2,1,0:T(8,128)(2,1)S(1)}, u32[]{:S(2)}, u32[]{:S(2)}) async-start(bf16[8,25,8,128]{3,2,1,0:T(8,128)(2,1)} %shard_map.97), calls=%async_computation.1 | async-start | bytes 819200 | tf_op jit(solution)/shard_map/all_to_all | solution.py:396
  27.8 34.3 %copy-start = (bf16[512,400]{0,1:T(8,128)(2,1)S(1)}, bf16[512,400]{0,1:T(8,128)(2,1)}, u32[]{:S(2)}) copy-start(bf16[512,400]{0,1:T(8,128)(2,1)} %param.8) | copy-start | bytes 1228804
  27.8 34.3 %copy-start.1 = (f32[400,128]{1,0:T(8,128)S(1)}, f32[400,128]{1,0:T(8,128)}, u32[]{:S(2)}) copy-start(f32[400,128]{1,0:T(8,128)} %shard_map.95.weights) | copy-start | bytes 614404
  27.8 34.3 %copy-start.3 = (s32[16,256]{1,0:T(8,128)S(1)}, s32[16,256]{1,0:T(8,128)}, u32[]{:S(2)}) copy-start(s32[16,256]{1,0:T(8,128)} %heads.3) | copy-start | bytes 49156
  49.4 1.3 %collective-permute-start = (bf16[7,8,128]{2,1,0:T(8,128)(2,1)S(1)}, bf16[7,8,128]{2,1,0:T(8,128)(2,1)S(1)}, u32[]{:S(2)}, u32[]{:S(2)}) collective-permute-start(bf16[7,8,128]{2,1,0:T(8,128)(2,1)S(1)} %slice_reduce_fusion), channel_id=1, source_target_pairs={{0,1},{1,0},{2,3},{3,2},{4,5},{5,4},{6,7},{7,6},{8,9},{9,8},{10,11... | collective-permute-start | bytes 43016 | tf_op jit(solution)/shard_map/ppermute | solution.py:404
  51.4 21.5 %all-to-all-start.3 = ((bf16[16,7,8,128]{3,2,1,0:T(8,128)(2,1)}), bf16[16,7,8,128]{3,2,1,0:T(8,128)(2,1)S(1)}, u32[]{:S(2)}, u32[]{:S(2)}) async-start(bf16[16,7,8,128]{3,2,1,0:T(8,128)(2,1)} %broadcast_in_dim.2), calls=%async_computation.3 | async-start | bytes 458752 | tf_op jit(solution)/shard_map/all_to_all | solution.py:408

commit v5 on v4

--- a/solution.py
+++ b/solution.py
@@ -68,7 +68,7 @@
         weights[...] = total
 
 
-def query_kernel(count, ent, heads, weights, query, out, sems):
+def query_kernel(count, ent, heads, weights, query, first, out, sems):
     live = count[0, 0]
     pairs = 2 * ((live + 3) // 4)
     half, edges = ent.shape[0] // 2, heads.shape[1]
@@ -87,6 +87,8 @@
             out[pair, k] = jnp.concatenate([hr * wr - hi * wi, hr * wi + hi * wr], axis=0).astype(BF)
         put(pair).start()
 
+    first[...] = out[0]
+
     @pl.loop(0, pairs)
     def _(pair):
         put(pair).wait()
@@ -106,7 +108,7 @@
     return found
 
 
-def tail_kernel(count, query, partner, hub, tails, pick, diff, grads, table, acc, qin, picks, diffs, moves, qsem, psem, dsem):
+def tail_kernel(count, query, first, partner, hub, tails, pick, diff, grads, table, acc, qin, picks, diffs, moves, qsem, psem, dsem):
     dim, rows = hub.shape[0], partner.shape[1]
     edges = tails.shape[1]
     live = count[0, 0]
@@ -124,10 +126,11 @@
         both = pl.ds(2 * pair, 2)
         return pltpu.make_async_copy(diffs.at[both], diff.at[both], dsem.at[pair])
 
-    @pl.loop(0, pairs)
+    @pl.loop(1, pairs)
     def _(pair):
         fetch(pair).start()
 
+    qin[:2] = first[...]
     table[:, :rows] = partner[:dim]
     table[:, rows:] = hub[...]
     acc[...] = jnp.zeros_like(acc)
@@ -149,10 +152,9 @@
     def _(quad):
         for slot in range(2):
             pair = 2 * quad + slot
-            fetch(pair).wait()
-
             @pl.when(pair >= 1)
             def _():
+                fetch(pair).wait()
                 put_pick(pair - 1, 1 - slot).wait()
 
             ats = [slice(k * edges, (k + 1) * edges) for k in range(2)]
@@ -314,17 +316,17 @@
     tiles, edges = head_index.shape
     return call(
         query_kernel,
-        shape((2 * tiles, dim, edges), BF),
+        [shape((2 * tiles, dim, edges), BF), shape((2, dim, edges), BF)],
         [SMEM, VMEM, VMEM, VMEM],
-        HBM,
+        [HBM, VMEM],
         2 * tiles * edges * dim * rows,
         2 * tiles * dim * edges,
         [pltpu.VMEM((tiles // 2, 2, dim, edges), BF), DMA((tiles // 2,))],
-        vmem=60,
+        vmem=50,
     )(tile_count, ent, head_index, weights)
 
 
-def run_tail(tile_count, query, partner, hub, tail_index, groups):
+def run_tail(tile_count, query, first, partner, hub, tail_index, groups):
     tiles, edges = tail_index.shape
     dim = query.shape[1]
     rows, hubs = partner.shape[1], hub.shape[1]
@@ -335,7 +337,7 @@
             shape((3 * tiles, edges, edges), BF),
             shape((groups, sum(sizes(dim, rows, hubs, groups)), 8, LANES), BF),
         ],
-        [SMEM, HBM, VMEM, VMEM, VMEM],
+        [SMEM, HBM, VMEM, VMEM, VMEM, VMEM],
         [HBM, HBM, VMEM],
         4 * tiles * edges * dim * (rows + hubs + edges),
         8 * tiles * dim * edges,
@@ -352,7 +354,7 @@
         ],
         tiles * edges * edges,
         vmem=50,
-    )(tile_count, query, partner, hub, tail_index)
+    )(tile_count, query, first, partner, hub, tail_index)
 
 
 def run_head(tile_count, pick, diff, weights, head_index, ent):
@@ -395,8 +397,8 @@
         )(matching, cut)
         partner = lax.all_to_all(cut, "group", 0, 0).reshape(high, wide, 8, LANES)
         partner = partner.transpose(0, 2, 1, 3).reshape(dim, rows)
-        query = run_query(tile_count, ent, head_index, weights)
-        pick, diff, grads = run_tail(tile_count, query, partner, hub, tail_index, groups)
+        query, first = run_query(tile_count, ent, head_index, weights)
+        pick, diff, grads = run_tail(tile_count, query, first, partner, hub, tail_index, groups)
 
         got = lax.all_to_all(grads, "group", 0, 0)
         got, pick, diff = lax.optimization_barrier((got, pick, diff))

time: 88.2 us -> 86.3 us (0.978)
  the two profiles are of different devices: /device:TPU:8 before, /device:TPU:64 now
where the time goes in v5:
time: 86.3 us; the launch traced here: 85.4 us
  blocking collectives  28.6 us (33%)
  Pallas kernels  19.2 us (22%)
  starting transfers between devices  17.6 us (20%)
  waiting for transfers between devices  16.9 us (20%)
  local copies, waits for them, and re-layouts  1.67 us (2%)
  between operations  1.42 us (2%)
    all_to_all x1, blocking collectives, shards(): got = lax.all_to_all(grads, 'group', 0, 0)  15.9 us
    all_to_all x1, blocking collectives, shards(): last = lax.all_to_all(sent, 'group', 0, 0)  12.7 us
    all_to_all x1, starting transfers between devices, shards(): parts = lax.all_to_all(parts, 'member', 0, 0, axis_index_groups=cores)  8.2 us
    all_to_all x1, waiting for transfers between devices, shards(): parts = lax.all_to_all(parts, 'member', 0, 0, axis_index_groups=cores)  7.44 us
    pallas_call x1, Pallas kernels, run_tail(): call(tail_kernel, [shape((tiles, dim, 2 * edges), BF), shape((3 * tiles,...  5.86 us
    all_to_all x1, starting transfers between devices, shards(): cut = lax.all_to_all(cut.reshape(groups, -1, 8, LANES), 'group', 0, 0)  5.8 us
    all_to_all x1, waiting for transfers between devices, shards(): partner = lax.all_to_all(cut, 'group', 0, 0).reshape(high, wide, 8, LANES)  4.54 us
    pallas_call x1, Pallas kernels, run_weights(): call(weight_kernel, shape((dim, LANES), F32), [SMEM, SMEM, HBM], VMEM, 40...  4.2 us
  transfers between devices with their start and end apart: 4, of which 4 were waited for; matrix products, arithmetic and copies ran while one was open for 0% of the time, Pallas kernels for 12%

profile of v5, /device:TPU:64, one launch (start us, length us, event | category | flops | bytes accessed | tf_op | source)
XLA Modules:
  0.0 85.4 jit_solution(9524911344226248780)
XLA Ops:
  0.6 0.0 copy-start
  0.6 0.0 copy-start.5
  0.7 5.8 %all-to-all-start = ((bf16[8,25,8,128]{3,2,1,0:T(8,128)(2,1)}), bf16[8,25,8,128]{3,2,1,0:T(8,128)(2,1)S(1)}, u32[]{:S(2)}, u32[]{:S(2)}) async-start(bf16[8,25,8,128]{3,2,1,0:T(8,128)(2,1)} %bitcast.16), calls=%async_computation | async-start | bytes 819200 | tf_op jit(solution)/shard_map/all_to_all | solution.py:392
  7.1 0.0 copy-start.3
  7.1 0.0 copy-start.6
  7.1 4.2 %shard_map.95.weights = f32[400,128]{1,0:T(8,128)} custom-call(s32[1,1]{1,0:T(1,128)S(6)} %copy.10.count, s32[16]{0:T(128)} %rel_ids.1, f32[400,2112]{1,0:T(8,128)} %bitcast.22), custom_call_target="tpu_custom_call" | custom-call | flops 2560000000 | bytes 3379200 | tf_op jit(solution)/shard_map/pallas_call | solution.py:302
  11.3 3.7 %all-to-all-done.rows = bf16[8,25,8,128]{3,2,1,0:T(8,128)(2,1)S(1)} async-done(((bf16[8,25,8,128]{3,2,1,0:T(8,128)(2,1)}), bf16[8,25,8,128]{3,2,1,0:T(8,128)(2,1)S(1)}, u32[]{:S(2)}, u32[]{:S(2)}) %all-to-all-start) | async-done | bytes 409632 | tf_op jit(solution)/shard_map/all_to_all | solution.py:392
  15.1 0.0 copy-done.5
  15.1 1.4 %shard_map.97 = bf16[8,25,8,128]{3,2,1,0:T(8,128)(2,1)} custom-call(s32[8]{0:T(128)S(1)} %copy-done.5, bf16[8,25,8,128]{3,2,1,0:T(8,128)(2,1)S(1)} %all-to-all-done.rows), custom_call_target="tpu_custom_call" | custom-call | bytes 819200 | tf_op jit(solution)/shard_map/pallas_call | solution.py:395
  16.4 3.5 %all-to-all-start.1 = ((bf16[8,25,8,128]{3,2,1,0:T(8,128)(2,1)}), bf16[8,25,8,128]{3,2,1,0:T(8,128)(2,1)S(1)}, u32[]{:S(2)}, u32[]{:S(2)}) async-start(bf16[8,25,8,128]{3,2,1,0:T(8,128)(2,1)} %shard_map.97), calls=%async_computation.1 | async-start | bytes 819200 | tf_op jit(solution)/shard_map/all_to_all | solution.py:398
  19.9 0.9 %copy-done.1 = f32[400,128]{1,0:T(8,128)S(1)} copy-done((f32[400,128]{1,0:T(8,128)S(1)}, f32[400,128]{1,0:T(8,128)}, u32[]{:S(2)}) %copy-start.1) | copy-done | bytes 204824
  20.9 2.6 %shard_map.96 = (bf16[32,400,256]{2,1,0:T(8,128)(2,1)}, bf16[2,400,256]{2,1,0:T(8,128)(2,1)S(1)}) custom-call(s32[1,1]{1,0:T(1,128)S(6)} %copy.10.count, bf16[400,512]{1,0:T(8,128)(2,1)S(1)} %bitcast.17, s32[16,256]{1,0:T(8,128)S(1)} %copy-done.4, f32[400,128]{1,0:T(8,128)S(1)} %copy-done.1), custom_call_target="tpu_custom_call" | custom-call | flops 1677721600 | bytes 3276800 | tf_op jit(solution)/shard_map/pallas_call | solution.py:317
  23.4 4.5 %all-to-all-done.1 = bf16[8,25,8,128]{3,2,1,0:T(8,128)(2,1)S(1)} async-done(((bf16[8,25,8,128]{3,2,1,0:T(8,128)(2,1)}), bf16[8,25,8,128]{3,2,1,0:T(8,128)(2,1)S(1)}, u32[]{:S(2)}, u32[]{:S(2)}) %all-to-all-start.1) | async-done | bytes 409632 | tf_op jit(solution)/shard_map/all_to_all | solution.py:398
  28.0 5.9 %shard_map.98 = (bf16[16,400,512]{2,1,0:T(8,128)(2,1)}, bf16[48,256,256]{2,1,0:T(8,128)(2,1)}, bf16[8,32,8,128]{3,2,1,0:T(8,128)(2,1)S(1)}) custom-call(s32[1,1]{1,0:T(1,128)S(6)} %copy.10.count, bf16[32,400,256]{2,1,0:T(8,128)(2,1)} %get-tuple-element.17.query, bf16[2,400,256]{2,1,0:T(8,128)(2,1)S(1)} %get-tuple-element.18.first, ...), custom_call_target="tpu_custom_call" | custom-call | flops 5872025600 | bytes 13107200 | tf_op jit(solution)/shard_map/pallas_call | solution.py:333
  33.9 15.9 %all_to_all.25.back = bf16[8,32,8,128]{3,2,1,0:T(8,128)(2,1)S(1)} all-to-all(bf16[8,32,8,128]{3,2,1,0:T(8,128)(2,1)S(1)} %get-tuple-element.20), channel_id=1, replica_groups=mesh['group'=8,'member'=32] {'group'}, dimensions={0} | all-to-all | bytes 1048576 | tf_op jit(solution)/shard_map/all_to_all | solution.py:403
  49.8 0.1 collective-permute-start
  49.9 1.2 %collective-permute-done = bf16[7,8,128]{2,1,0:T(8,128)(2,1)S(1)} collective-permute-done((bf16[7,8,128]{2,1,0:T(8,128)(2,1)S(1)}, bf16[7,8,128]{2,1,0:T(8,128)(2,1)S(1)}, u32[]{:S(2)}, u32[]{:S(2)}) %collective-permute-start) | collective-permute-done | bytes 14368 | tf_op jit(solution)/shard_map/ppermute | solution.py:406
  51.1 0.7 broadcast_in_dim.2
  51.8 8.2 %all-to-all-start.3 = ((bf16[16,7,8,128]{3,2,1,0:T(8,128)(2,1)}), bf16[16,7,8,128]{3,2,1,0:T(8,128)(2,1)S(1)}, u32[]{:S(2)}, u32[]{:S(2)}) async-start(bf16[16,7,8,128]{3,2,1,0:T(8,128)(2,1)} %broadcast_in_dim.2), calls=%async_computation.3 | async-start | bytes 458752 | tf_op jit(solution)/shard_map/all_to_all | solution.py:410
  60.0 3.7 %shard_map.99.base = f32[400,512]{1,0:T(8,128)S(1)} custom-call(s32[1,1]{1,0:T(1,128)S(6)} %copy.10.count, bf16[16,400,512]{2,1,0:T(8,128)(2,1)} %get-tuple-element.24.pick, bf16[48,256,256]{2,1,0:T(8,128)(2,1)} %get-tuple-element.25.diff, f32[400,128]{1,0:T(8,128)S(1)} %copy-done.2, s32[16,256]{1,0:T(8,128)S(1)} %copy-done.4, bf16[400,512]{1,0:T(8,128)(2,1)S(1)} %bitcast.18), custom_call_target="tpu_custom_call" | custom-call | flops 2516582400 | bytes 9830400 | tf_op jit(solution)/shard_map/pallas_call | solution.py:363
  63.7 7.4 %all-to-all-done.3.hub = bf16[16,7,8,128]{3,2,1,0:T(8,128)(2,1)S(1)} async-done(((bf16[16,7,8,128]{3,2,1,0:T(8,128)(2,1)}), bf16[16,7,8,128]{3,2,1,0:T(8,128)(2,1)S(1)}, u32[]{:S(2)}, u32[]{:S(2)}) %all-to-all-start.3) | async-done | bytes 229408 | tf_op jit(solution)/shard_map/all_to_all | solution.py:410
  71.1 0.6 shard_map.100
  71.7 12.7 %all_to_all.26.last = bf16[8,32,8,128]{3,2,1,0:T(8,128)(2,1)S(1)} all-to-all(bf16[8,32,8,128]{3,2,1,0:T(8,128)(2,1)S(1)} %shard_map.100), channel_id=1, replica_groups=mesh['group'=8,'member'=32] {'group'}, dimensions={0} | all-to-all | bytes 1048576 | tf_op jit(solution)/shard_map/all_to_all | solution.py:416
  84.4 0.9 %shard_map.101 = (bf16[400,512]{1,0:T(8,128)(2,1)}, bf16[400,128]{1,0:T(8,128)(2,1)}) custom-call(f32[400,512]{1,0:T(8,128)S(1)} %shard_map.99.base, bf16[400,128]{1,0:T(8,128)(2,1)S(1)} %bitcast.21, bf16[8,32,8,128]{3,2,1,0:T(8,128)(2,1)S(1)} %all_to_all.26.last), custom_call_target="tpu_custom_call" | custom-call | bytes 1638400 | tf_op jit(solution)/shard_map/pallas_call | solution.py:417
  (10 shorter events, 0.0 us)
Async XLA Ops:
  0.6 19.3 %copy-start = (bf16[512,400]{0,1:T(8,128)(2,1)S(1)}, bf16[512,400]{0,1:T(8,128)(2,1)}, u32[]{:S(2)}) copy-start(bf16[512,400]{0,1:T(8,128)(2,1)} %param.8) | copy-start | bytes 1228804
  0.6 14.4 %copy-start.5 = (s32[8]{0:T(128)S(1)}, s32[8]{0:T(128)}, u32[]{:S(2)}) copy-start(s32[8]{0:T(128)} %matching.3) | copy-start | bytes 100
  0.6 19.3 %copy-start.4 = (s32[16,256]{1,0:T(8,128)S(1)}, s32[16,256]{1,0:T(8,128)}, u32[]{:S(2)}) copy-start(s32[16,256]{1,0:T(8,128)} %heads.3) | copy-start | bytes 49156
  0.7 14.4 %all-to-all-start = ((bf16[8,25,8,128]{3,2,1,0:T(8,128)(2,1)}), bf16[8,25,8,128]{3,2,1,0:T(8,128)(2,1)S(1)}, u32[]{:S(2)}, u32[]{:S(2)}) async-start(bf16[8,25,8,128]{3,2,1,0:T(8,128)(2,1)} %bitcast.16), calls=%async_computation | async-start | bytes 819200 | tf_op jit(solution)/shard_map/all_to_all | solution.py:392
  7.1 20.9 %copy-start.3 = (bf16[128,400]{0,1:T(8,128)(2,1)S(1)}, bf16[128,400]{0,1:T(8,128)(2,1)}, u32[]{:S(2)}) copy-start(bf16[128,400]{0,1:T(8,128)(2,1)} %param.9) | copy-start | bytes 307204
  7.1 20.9 %copy-start.6 = (s32[16,256]{1,0:T(8,128)S(1)}, s32[16,256]{1,0:T(8,128)}, u32[]{:S(2)}) copy-start(s32[16,256]{1,0:T(8,128)} %tails.1) | copy-start | bytes 49156
  16.4 11.6 %all-to-all-start.1 = ((bf16[8,25,8,128]{3,2,1,0:T(8,128)(2,1)}), bf16[8,25,8,128]{3,2,1,0:T(8,128)(2,1)S(1)}, u32[]{:S(2)}, u32[]{:S(2)}) async-start(bf16[8,25,8,128]{3,2,1,0:T(8,128)(2,1)} %shard_map.97), calls=%async_computation.1 | async-start | bytes 819200 | tf_op jit(solution)/shard_map/all_to_all | solution.py:398
  19.9 0.9 %copy-start.1 = (f32[400,128]{1,0:T(8,128)S(1)}, f32[400,128]{1,0:T(8,128)}, u32[]{:S(2)}) copy-start(f32[400,128]{1,0:T(8,128)} %shard_map.95.weights) | copy-start | bytes 614404
  28.0 32.0 %copy-start.2 = (f32[400,128]{1,0:T(8,128)S(1)}, f32[400,128]{1,0:T(8,128)}, u32[]{:S(2)}) copy-start(f32[400,128]{1,0:T(8,128)} %shard_map.95.weights) | copy-start | bytes 614404
  49.8 1.3 %collective-permute-start = (bf16[7,8,128]{2,1,0:T(8,128)(2,1)S(1)}, bf16[7,8,128]{2,1,0:T(8,128)(2,1)S(1)}, u32[]{:S(2)}, u32[]{:S(2)}) collective-permute-start(bf16[7,8,128]{2,1,0:T(8,128)(2,1)S(1)} %slice_reduce_fusion), channel_id=1, source_target_pairs={{0,1},{1,0},{2,3},{3,2},{4,5},{5,4},{6,7},{7,6},{8,9},{9,8},{10,11... | collective-permute-start | bytes 43016 | tf_op jit(solution)/shard_map/ppermute | solution.py:406
  51.8 19.3 %all-to-all-start.3 = ((bf16[16,7,8,128]{3,2,1,0:T(8,128)(2,1)}), bf16[16,7,8,128]{3,2,1,0:T(8,128)(2,1)S(1)}, u32[]{:S(2)}, u32[]{:S(2)}) async-start(bf16[16,7,8,128]{3,2,1,0:T(8,128)(2,1)} %broadcast_in_dim.2), calls=%async_computation.3 | async-start | bytes 458752 | tf_op jit(solution)/shard_map/all_to_all | solution.py:410
